TPU v7x, 32 devices: a whole 2x2x4 slice. The times are simulated.
32 devices in a mesh: seq: 8 (over z, core), head: 4 (over y, x).
Axes of the slice: x: 2, y: 2, z: 4, core: 2. Of those that a mesh axis runs over, the one named last changes fastest.
Arguments:
- tokens: bfloat16 [4096, 2304], P(('seq', 'head')), may hold values from -6 to 6
- in_gain: float32 [2304], replicated, may hold values from 0.5 to 1.5
- out_gain: float32 [2304], replicated, may hold values from 0.5 to 1.5
- query_weight: bfloat16 [2304, 2048], P(None, 'head'), may hold values from -1.25 to 1.25
- keyval_weight: bfloat16 [2304, 2048], replicated, may hold values from -0.125 to 0.125
- out_weight: bfloat16 [2048, 2304], P('head'), may hold values from -0.125 to 0.125
- cache_entries: bfloat16 [4, 2048, 512], P(None, 'seq'), may hold values from -6 to 6
- segment_ids: int32 [4096], P('seq'), may hold values from -1 to 63, as said below
- cache_lengths: int32 [64], replicated, may hold values from 0 to 512, as said below
- block_owners: int32 [128], P('seq'), may hold values from -1 to 63, as said below
Outputs:
- layer_out: bfloat16 [4096, 2304], P(('seq', 'head'))
Inputs may be any that keep to these rules, and one draw needn't show every extreme that they name: `segment_ids`: valid slots come first and their ids never fall; every id from 0 to 63 has at least one slot; padding slots, marked -1, fill the end of the stream; exactly one segment has 2048 slots and none has more. `block_owners`: the segment that owns each cache block, or -1 for a free block; a segment's cache fills its blocks in the order of their indices; no segment owns more than 32 blocks. `cache_lengths`: zero for a segment without blocks, and some segment has none; otherwise more than 16 times one less than its number of blocks and at most 16 times that number; exactly one segment holds 512 rows.
All inputs are finite; a program needn't handle non-finite values.
Results may differ from a plain program's by a relative error of at most 0.012.
Values may be sent and summed in bfloat16 or wider, within the bound.
A program may use at most 128 MiB of HBM per device.

v0:
```python
import math

import jax
import jax.numpy as jnp
from jax import lax
from jax.sharding import PartitionSpec as P

QH = 8
KVH = 4
HD = 256
NSEG = 64
BLK = 16


EPSILON = 1e-06
SOFT_CAP = 50.0


def carried_in(array, axis, combine, identity):
    devices, position = (lax.axis_size(axis), lax.axis_index(axis))
    everything = jax.tree.map(lambda part: lax.all_gather(part, axis), array)
    start = jax.tree.map(
        lambda part, zero: jnp.broadcast_to(jnp.asarray(zero, part.dtype), part.shape),
        array,
        identity,
    )

    def hop(k, before):
        reached = k < position
        new = combine(before, jax.tree.map(lambda part: part[k], everything))
        return jax.tree.map(lambda a, b: jnp.where(reached, a, b), new, before)

    return lax.fori_loop(0, devices, hop, start)


def rms_scale(matrix, scaling):
    matrix = matrix.astype(jnp.float32)
    mean_square = jnp.mean(matrix * matrix, axis=-1, keepdims=True)
    return matrix * lax.rsqrt(mean_square + EPSILON) * scaling


def frequencies(extent):
    return 10000.0 ** (-(jnp.arange(extent // 2, dtype=jnp.float32) * 2.0 / extent))


def rotate(vectors, angles):
    half_width = vectors.shape[-1] // 2
    leading = vectors[..., :half_width]
    trailing = vectors[..., half_width:]
    cosine = jnp.cos(angles)
    sine_part = jnp.sin(angles)
    return jnp.concatenate(
        [leading * cosine - trailing * sine_part, trailing * cosine + leading * sine_part], axis=-1
    )


def attention_fold(queries, q_seg, q_slot, key_width):
    present = q_seg >= 0

    def advance(totals, key_block):
        pair_rows, key_seg, key_slot = key_block
        numerator, denominator = totals
        scores = jnp.einsum(
            "qhd,kd->qhk", queries, pair_rows[:, :key_width], preferred_element_type=jnp.float32
        )
        scores = SOFT_CAP * jnp.tanh(scores / SOFT_CAP)
        allowed = (
            (key_seg[None, :] == q_seg[:, None])
            & (key_slot[None, :] <= q_slot[:, None])
            & present[:, None]
        )
        weights = jnp.where(allowed[:, None, :], jnp.exp(scores), 0.0)
        denominator = denominator + jnp.sum(weights, axis=-1)
        numerator = numerator + jnp.einsum(
            "qhk,kd->qhd",
            weights.astype(jnp.bfloat16),
            pair_rows[:, key_width:],
            preferred_element_type=jnp.float32,
        )
        return ((numerator, denominator), None)

    def folding(totals, portion, offset):
        pair_rows, key_seg, key_slot = portion
        row_count = pair_rows.shape[0]
        block_rows = math.gcd(row_count, 1024)
        block_count = row_count // block_rows
        blocks = (
            pair_rows.reshape(block_count, block_rows, pair_rows.shape[1]),
            key_seg.reshape(block_count, block_rows),
            key_slot.reshape(block_count, block_rows),
        )
        totals, _ = lax.scan(advance, totals, blocks)
        return totals

    return folding


def local(
    tokens,
    in_gain,
    out_gain,
    query_weight,
    keyval_weight,
    out_weight,
    cache_entries,
    segment_ids,
    cache_lengths,
    block_owners,
):
    heads_here = query_weight.shape[1] // HD
    group_size = QH // KVH
    seq_index = lax.axis_index("seq")
    head_index = lax.axis_index("head")
    shared_head = head_index * heads_here // group_size
    stream_rows = segment_ids.shape[0]
    seg_range = jnp.arange(NSEG, dtype=jnp.int32)
    matches = (segment_ids[:, None] == seg_range[None, :]).astype(jnp.int32)
    counts = jnp.sum(matches, axis=0)
    owner_match = (block_owners[:, None] == seg_range[None, :]).astype(jnp.int32)
    owned_count = jnp.sum(owner_match, axis=0)

    def add_pairs(earlier, later):
        return (earlier[0] + later[0], earlier[1] + later[1])

    empty_counts = jnp.zeros((NSEG,), jnp.int32)
    before_tokens, before_blocks = carried_in(
        (counts, owned_count), "seq", add_pairs, (empty_counts, empty_counts)
    )
    first_local = jnp.cumsum(counts) - counts
    local_slot = jnp.arange(stream_rows, dtype=jnp.int32)
    positions = (
        jnp.sum(matches * (cache_lengths + before_tokens - first_local)[None, :], axis=1)
        + local_slot
    )
    q_slot = seq_index * stream_rows + local_slot
    angles_all = positions.astype(jnp.float32)[:, None] * frequencies(HD)[None, :]
    block_rank = jnp.sum(
        owner_match * (jnp.cumsum(owner_match, axis=0) - owner_match + before_blocks[None, :]),
        axis=1,
    )
    limits = jnp.sum(owner_match * cache_lengths[None, :], axis=1)
    offsets = jnp.arange(BLK, dtype=jnp.int32)
    usable = (block_owners[:, None] >= 0) & (
        block_rank[:, None] * BLK + offsets[None, :] < limits[:, None]
    )
    cache_seg = jnp.where(usable, block_owners[:, None], -1).reshape(-1)
    cache_pairs = lax.dynamic_index_in_dim(cache_entries, shared_head, 0, keepdims=False)
    cache_slot = jnp.full((cache_seg.shape[0],), -1, jnp.int32)
    w_shared = lax.dynamic_slice_in_dim(keyval_weight, shared_head * 2 * HD, 2 * HD, 1)
    portion = lax.all_gather(tokens, "head", axis=0, tiled=True)
    row_count = portion.shape[0]
    normed = rms_scale(portion, in_gain).astype(jnp.bfloat16)
    query_rows = jnp.dot(normed, query_weight, preferred_element_type=jnp.float32).reshape(
        row_count, heads_here, HD
    )
    query_rows = (rotate(query_rows, angles_all[:, None, :]) * HD ** (-0.5)).astype(jnp.bfloat16)
    keyval = jnp.dot(normed, w_shared, preferred_element_type=jnp.float32)
    key_rows = rotate(keyval[:, :HD], angles_all).astype(jnp.bfloat16)
    value_rows = keyval[:, HD:].astype(jnp.bfloat16)
    projected = jnp.concatenate(
        [query_rows.reshape(row_count, heads_here * HD), key_rows, value_rows], axis=1
    )
    queries = projected[:, : heads_here * HD].reshape(stream_rows, heads_here, HD)
    new_pairs = projected[:, heads_here * HD :]
    folding = attention_fold(queries, segment_ids, q_slot, HD)
    start_totals = (
        jnp.zeros((stream_rows, heads_here, HD), jnp.float32),
        jnp.zeros((stream_rows, heads_here), jnp.float32),
    )
    partial_value = folding(
        start_totals,
        (
            lax.all_gather(new_pairs, "seq", axis=0, tiled=True),
            lax.all_gather(segment_ids, "seq", axis=0, tiled=True),
            lax.all_gather(q_slot, "seq", axis=0, tiled=True),
        ),
        jnp.int32(0),
    )
    numerator, denominator = folding(
        partial_value,
        (
            lax.all_gather(cache_pairs, "seq", axis=0, tiled=True),
            lax.all_gather(cache_seg, "seq", axis=0, tiled=True),
            lax.all_gather(cache_slot, "seq", axis=0, tiled=True),
        ),
        jnp.int32(0),
    )
    present = segment_ids >= 0
    safe = jnp.where(present[:, None], denominator, 1.0)
    attended = jnp.where(present[:, None, None], numerator / safe[:, :, None], 0.0)
    attended = attended.astype(jnp.bfloat16).reshape(stream_rows, heads_here * HD)
    branch = lax.psum_scatter(
        jnp.dot(attended, out_weight, preferred_element_type=jnp.float32),
        "head",
        scatter_dimension=0,
        tiled=True,
    )
    return (tokens.astype(jnp.float32) + rms_scale(branch, out_gain)).astype(jnp.bfloat16)


def solution(mesh):
    in_specs = (
        P(("seq", "head"), None),
        P(),
        P(),
        P(None, "head"),
        P(),
        P("head", None),
        P(None, "seq", None),
        P("seq"),
        P(),
        P("seq"),
    )
    out_specs = P(("seq", "head"), None)
    return jax.shard_map(local, mesh=mesh, in_specs=in_specs, out_specs=out_specs, check_vma=False)
```

profile of v0, /device:TPU:16, one launch (start us, length us, event | category | flops | bytes accessed | tf_op | source)
XLA Modules:
  0.0 245.2 jit_solution(8027556891641300505)
XLA Ops:
  6.5 0.7 all-gather.10.cloned.1.call-update
  7.4 1.2 dynamic-slice
  9.2 0.8 convert_reduce_fusion
  10.0 0.2 dynamic-update-slice
  10.2 0.7 fusion.40
  11.0 0.2 dynamic-update-slice.1
  11.2 6.9 %all-reduce.2 = (s32[512]{0:T(512)S(1)}, s32[512]{0:T(512)S(1)}) all-reduce(s32[512]{0:T(512)S(1)} %dynamic-update-slice, s32[512]{0:T(512)S(1)} %dynamic-update-slice.1), channel_id=2, replica_groups=mesh['seq'=8,'head'=4] {'seq'}, use_global_device_ids=true, to_apply=%add | all-reduce | flops 1024 | bytes 8192
  18.6 0.3 while.44
  18.9 0.7 subtract_subtract_fusion
  19.6 0.8 select_reduce_fusion
  20.4 27.4 %all-gather.10.cloned.1.call-done = bf16[512,2304]{1,0:T(8,128)(2,1)} async-done(((bf16[128,2304]{1,0:T(8,128)(2,1)}), bf16[512,2304]{1,0:T(8,128)(2,1)}) %all-gather.10.cloned.1.call-update) | async-done | bytes 2359312 | tf_op jit(solution)/shard_map/all_gather | solution.py:150
  47.8 2.2 fusion.28
  50.0 3.9 %fusion.31 = f32[512,512]{0,1:T(8,128)S(1)} fusion(bf16[2304,2048]{1,0:T(8,128)(2,1)} %param.20, s32[]{:T(128)S(6)} %select_n.68, bf16[512,2304]{1,0:T(8,128)(2,1)} %all-gather.10.cloned.1.call-done, f32[2304]{0:T(1024)} %param.17, f32[512]{0:T(512)S(1)} %add_rsqrt_fusion), kind=kOutput, calls=%fused_computation.45 | convolution fusion | flops 1212678144 | bytes 5781508 | tf_op jit(solution)/shard_map/dot_general | solution.py:157
  54.0 1.2 multiply_cosine_fusion
  55.2 0.8 pad_maximum_fusion
  56.1 1.7 constant_dynamic-slice_fusion.3
  58.0 11.3 %all-gather.4 = s32[8,1,512]{2,1,0:T(1,128)S(1)} all-gather(s32[1,1,512]{2,1,0:T(1,128)S(1)} %bitcast.98), channel_id=1, replica_groups=mesh['seq'=8,'head'=4] {'seq'}, dimensions={0}, use_global_device_ids=true | all-gather | bytes 18432 | tf_op jit(solution)/shard_map/all_gather | solution.py:175
  69.3 12.9 %all-gather.3 = s32[8,1,512]{2,1,0:T(1,128)S(1)} all-gather(s32[1,1,512]{2,1,0:T(1,128)S(1)} %bitcast.97), channel_id=1, replica_groups=mesh['seq'=8,'head'=4] {'seq'}, dimensions={0}, use_global_device_ids=true | all-gather | bytes 18432 | tf_op jit(solution)/shard_map/all_gather | solution.py:174
  82.3 0.2 select_reduce_fusion.2
  82.6 8.2 %all-gather.5 = s32[8,1,256]{2,1,0:T(1,128)S(1)} all-gather(s32[1,1,256]{2,1,0:T(1,128)S(1)} %reshape.296), channel_id=1, replica_groups=mesh['seq'=8,'head'=4] {'seq'}, dimensions={0}, use_global_device_ids=true | all-gather | bytes 9216 | tf_op jit(solution)/shard_map/all_gather | solution.py:183
  90.9 0.8 copy.41
  91.7 0.8 copy.43
  92.6 3.9 %fusion.34 = f32[512,512]{0,1:T(8,128)S(1)} fusion(bf16[2304,512]{1,0:T(8,128)(2,1)} %param.19, bf16[512,2304]{1,0:T(8,128)(2,1)} %all-gather.10.cloned.1.call-done, f32[2304]{0:T(1024)S(1)} %copy-done.9, f32[512]{0:T(512)S(1)} %add_rsqrt_fusion), kind=kOutput, calls=%fused_computation.52 | convolution fusion | flops 1212678144 | bytes 5778432 | tf_op jit(solution)/shard_map/dot_general | solution.py:153
  96.5 0.9 fusion.42
  97.4 0.2 copy.49
  97.6 1.2 copy.50
  98.8 1.2 multiply_subtract_fusion
  100.0 0.9 fusion.33
  100.8 1.5 all-gather.12.cloned.1.call-done
  102.4 6.5 %copy.48 = bf16[4096,512]{1,0:T(8,128)(2,1)} copy(bf16[4096,512]{0,1:T(8,128)(2,1)} %all-gather.12.cloned.1.call-done) | data formatting | bytes 8388608
  108.8 48.7 %while.45 = (s32[]{:T(128)}, f32[512,2,256]{2,0,1:T(8,128)}, f32[512,2]{0,1:T(2,128)S(1)}, s32[4,1024]{1,0:T(4,128)S(1)}, s32[512]{0:T(512)S(1)}, /*index=5*/s32...) while((s32[]{:T(128)}, f32[512,2,256]{2,0,1:T(8,128)}, ...), condition=%wide.region_9.10_spmd.clone, body=%wide.region_7.9_spmd.clone.sunk | while | flops 1084753408 | bytes 17873576 | solution.py:92
  108.9 1.1 and_and_fusion.5
  109.9 1.5 dynamic-slice_bitcast_fusion.5
  111.5 4.5 %fusion.63 = (f32[512,2]{0,1:T(2,128)S(1)}, f32[1024,512,2]{1,0,2:T(8,128)}) fusion(pred[512,1024]{0,1:T(8,128)(4,1)S(1)} %and_and_fusion.5, bf16[512,2,256]{2,0,1:T(8,128)(2,1)} %get-tuple-element.669, bf16[1024,512]{1,0:T(8,128)(2,1)S(1)} %dynamic-slice_bitcast_fusion.5), kind=kOutput, calls=%fused_computation.23.clone.1 | convolution fusion | flops 541064192 | bytes 5771264 | tf_op jit(solution)/shard_map/while/body/eval_jaxpr/qhd,kd->qhk/dot_general | solution.py:63
  116.0 4.8 %fusion.64 = f32[512,2,256]{2,0,1:T(8,128)} fusion(f32[1024,512,2]{1,0,2:T(8,128)} %get-tuple-element.611, pred[512,1024]{0,1:T(8,128)(4,1)} %copy-done.1, f32[512,2,256]{2,0,1:T(8,128)} %get-tuple-element.650, bf16[1024,512]{1,0:T(8,128)(2,1)S(1)} %dynamic-slice_bitcast_fusion.5, pred[]{:T(512)S(6)} %compare.9), kind=kOutput, calls=%fused_computation.28.clone.1 | convolution fusion | flops 541589504 | bytes 7340033 | tf_op jit(solution)/shard_map/while/body/eval_jaxpr/qhk,kd->qhd/dot_general | solution.py:74
  120.8 1.1 and_and_fusion.5
  121.9 1.5 dynamic-slice_bitcast_fusion.5
  123.4 4.5 %fusion.63 = (f32[512,2]{0,1:T(2,128)S(1)}, f32[1024,512,2]{1,0,2:T(8,128)}) fusion(pred[512,1024]{0,1:T(8,128)(4,1)S(1)} %and_and_fusion.5, bf16[512,2,256]{2,0,1:T(8,128)(2,1)} %get-tuple-element.669, bf16[1024,512]{1,0:T(8,128)(2,1)S(1)} %dynamic-slice_bitcast_fusion.5), kind=kOutput, calls=%fused_computation.23.clone.1 | convolution fusion | flops 541064192 | bytes 5771264 | tf_op jit(solution)/shard_map/while/body/eval_jaxpr/qhd,kd->qhk/dot_general | solution.py:63
  128.0 5.1 %fusion.64 = f32[512,2,256]{2,0,1:T(8,128)} fusion(f32[1024,512,2]{1,0,2:T(8,128)} %get-tuple-element.611, pred[512,1024]{0,1:T(8,128)(4,1)} %copy-done.1, f32[512,2,256]{2,0,1:T(8,128)} %get-tuple-element.650, bf16[1024,512]{1,0:T(8,128)(2,1)S(1)} %dynamic-slice_bitcast_fusion.5, pred[]{:T(512)S(6)} %compare.9), kind=kOutput, calls=%fused_computation.28.clone.1 | convolution fusion | flops 541589504 | bytes 7340033 | tf_op jit(solution)/shard_map/while/body/eval_jaxpr/qhk,kd->qhd/dot_general | solution.py:74
  133.1 1.1 and_and_fusion.5
  134.2 1.5 dynamic-slice_bitcast_fusion.5
  135.7 4.5 %fusion.63 = (f32[512,2]{0,1:T(2,128)S(1)}, f32[1024,512,2]{1,0,2:T(8,128)}) fusion(pred[512,1024]{0,1:T(8,128)(4,1)S(1)} %and_and_fusion.5, bf16[512,2,256]{2,0,1:T(8,128)(2,1)} %get-tuple-element.669, bf16[1024,512]{1,0:T(8,128)(2,1)S(1)} %dynamic-slice_bitcast_fusion.5), kind=kOutput, calls=%fused_computation.23.clone.1 | convolution fusion | flops 541064192 | bytes 5771264 | tf_op jit(solution)/shard_map/while/body/eval_jaxpr/qhd,kd->qhk/dot_general | solution.py:63
  140.2 5.1 %fusion.64 = f32[512,2,256]{2,0,1:T(8,128)} fusion(f32[1024,512,2]{1,0,2:T(8,128)} %get-tuple-element.611, pred[512,1024]{0,1:T(8,128)(4,1)} %copy-done.1, f32[512,2,256]{2,0,1:T(8,128)} %get-tuple-element.650, bf16[1024,512]{1,0:T(8,128)(2,1)S(1)} %dynamic-slice_bitcast_fusion.5, pred[]{:T(512)S(6)} %compare.9), kind=kOutput, calls=%fused_computation.28.clone.1 | convolution fusion | flops 541589504 | bytes 7340033 | tf_op jit(solution)/shard_map/while/body/eval_jaxpr/qhk,kd->qhd/dot_general | solution.py:74
  145.3 1.1 and_and_fusion.5
  146.4 1.5 dynamic-slice_bitcast_fusion.5
  147.9 4.5 %fusion.63 = (f32[512,2]{0,1:T(2,128)S(1)}, f32[1024,512,2]{1,0,2:T(8,128)}) fusion(pred[512,1024]{0,1:T(8,128)(4,1)S(1)} %and_and_fusion.5, bf16[512,2,256]{2,0,1:T(8,128)(2,1)} %get-tuple-element.669, bf16[1024,512]{1,0:T(8,128)(2,1)S(1)} %dynamic-slice_bitcast_fusion.5), kind=kOutput, calls=%fused_computation.23.clone.1 | convolution fusion | flops 541064192 | bytes 5771264 | tf_op jit(solution)/shard_map/while/body/eval_jaxpr/qhd,kd->qhk/dot_general | solution.py:63
  152.5 5.1 %fusion.64 = f32[512,2,256]{2,0,1:T(8,128)} fusion(f32[1024,512,2]{1,0,2:T(8,128)} %get-tuple-element.611, pred[512,1024]{0,1:T(8,128)(4,1)} %copy-done.1, f32[512,2,256]{2,0,1:T(8,128)} %get-tuple-element.650, bf16[1024,512]{1,0:T(8,128)(2,1)S(1)} %dynamic-slice_bitcast_fusion.5, pred[]{:T(512)S(6)} %compare.9), kind=kOutput, calls=%fused_computation.28.clone.1 | convolution fusion | flops 541589504 | bytes 7340033 | tf_op jit(solution)/shard_map/while/body/eval_jaxpr/qhk,kd->qhd/dot_general | solution.py:74
  157.6 14.8 %while.43 = (s32[]{:T(128)}, f32[512,2,256]{2,0,1:T(8,128)}, f32[512,2]{0,1:T(2,128)S(1)}, s32[2,1024]{1,0:T(2,128)S(1)}, s32[512]{0:T(512)S(1)}, /*index=5*/pre...) while((s32[]{:T(128)}, f32[512,2,256]{2,0,1:T(8,128)}, ...), condition=%wide.region_15.16_spmd.clone, body=%wide.region_13.15_spmd.clone.sunk | while | flops 1083966464 | bytes 24149672 | solution.py:92
  157.6 0.5 and_and_fusion.4
  158.1 1.3 dynamic-slice_bitcast_fusion.4
  159.4 2.7 %fusion.59 = (f32[512,2]{0,1:T(2,128)S(1)}, f32[1024,512,2]{1,0,2:T(8,128)S(1)}) fusion(pred[512,1024]{0,1:T(8,128)(4,1)S(1)} %and_and_fusion.4, bf16[512,2,256]{2,0,1:T(8,128)(2,1)} %get-tuple-element.700, bf16[1024,512]{1,0:T(8,128)(2,1)S(1)} %dynamic-slice_bitcast_fusion.4), kind=kOutput, calls=%fused_computation.3.clone.1 | convolution fusion | flops 541064192 | bytes 5771264 | tf_op jit(solution)/shard_map/while/body/eval_jaxpr/qhd,kd->qhk/dot_general | solution.py:63
  162.2 1.8 fusion.60
  164.0 0.9 copy-done.4
  165.0 0.5 and_and_fusion.4
  165.5 1.3 dynamic-slice_bitcast_fusion.4
  166.8 2.7 %fusion.59 = (f32[512,2]{0,1:T(2,128)S(1)}, f32[1024,512,2]{1,0,2:T(8,128)S(1)}) fusion(pred[512,1024]{0,1:T(8,128)(4,1)S(1)} %and_and_fusion.4, bf16[512,2,256]{2,0,1:T(8,128)(2,1)} %get-tuple-element.700, bf16[1024,512]{1,0:T(8,128)(2,1)S(1)} %dynamic-slice_bitcast_fusion.4), kind=kOutput, calls=%fused_computation.3.clone.1 | convolution fusion | flops 541064192 | bytes 5771264 | tf_op jit(solution)/shard_map/while/body/eval_jaxpr/qhd,kd->qhk/dot_general | solution.py:63
  169.6 1.9 fusion.60
  171.4 0.9 copy-done.4
  172.4 1.6 copy.45
  174.0 0.1 select_convert_fusion
  174.1 3.5 %fusion.43 = f32[512,2304]{1,0:T(8,128)} fusion(bf16[512,512]{0,1:T(8,128)(2,1)S(1)} %bitcast.92, bf16[512,2304]{1,0:T(8,128)(2,1)S(1)} %copy-done), kind=kOutput, calls=%fused_computation.85 | convolution fusion | flops 1207959552 | bytes 7602176 | tf_op jit(solution)/shard_map/dot_general | solution.py:193
  177.7 57.1 %reduce-scatter.2.cloned.1.call-done = f32[128,2304]{1,0:T(8,128)} async-done(((f32[512,2304]{1,0:T(8,128)}), f32[128,2304]{1,0:T(8,128)}) %reduce-scatter.2.cloned.1.call-update) | async-done | bytes 1179664 | tf_op jit(solution)/shard_map/reduce_scatter | solution.py:192
  234.8 1.4 multiply_reduce_fusion
  236.3 2.3 add_convert_fusion
  (93 shorter events, 1.5 us)
Async XLA Ops:
  6.5 167.6 %copy-start = (bf16[512,2304]{1,0:T(8,128)(2,1)S(1)}, bf16[512,2304]{1,0:T(8,128)(2,1)}, u32[]{:S(2)}) copy-start(bf16[512,2304]{1,0:T(8,128)(2,1)} %param.21) | copy-start | bytes 7077892
  6.5 41.2 %all-gather.10.cloned.1.call-start = ((), (), s32[]{:S(2)}) async-start(), calls=%async_computation.1 | async-start | bytes 2949120 | tf_op jit(solution)/shard_map/all_gather | solution.py:150
  7.3 95.1 %all-gather.12.cloned.1.call-start = ((), (), s32[]{:S(2)}) async-start(), calls=%async_computation.2 | async-start | bytes 4718592 | tf_op jit(solution)/shard_map/all_gather | solution.py:173
  53.9 3.9 %copy-start.5 = (s32[512]{0:T(512)S(1)}, s32[512]{0:T(512)}, u32[]{:S(2)}) copy-start(s32[512]{0:T(512)} %param.23) | copy-start | bytes 6148
  53.9 4.0 %copy-start.7 = (s32[16]{0:T(128)S(1)}, s32[16]{0:T(128)}, u32[]{:S(2)}) copy-start(s32[16]{0:T(128)} %param.25) | copy-start | bytes 196
  53.9 28.4 %copy-start.8 = (s32[64]{0:T(128)S(1)}, s32[64]{0:T(128)}, u32[]{:S(2)}) copy-start(s32[64]{0:T(128)} %param.24) | copy-start | bytes 772
  53.9 38.6 %copy-start.9 = (f32[2304]{0:T(1024)S(1)}, f32[2304]{0:T(1024)}, u32[]{:S(2)}) copy-start(f32[2304]{0:T(1024)} %param.17) | copy-start | bytes 27652
  56.0 101.5 %all-gather.14.cloned.1.call-start = ((), (), s32[]{:S(2)}) async-start(), calls=%async_computation.4 | async-start | bytes 2359296 | tf_op jit(solution)/shard_map/all_gather | solution.py:182
  57.8 177.0 %reduce-scatter.2.cloned.1.call-start = ((), (), s32[]{:S(2)}) async-start(), calls=%async_computation.3 | async-start | bytes 5898240 | tf_op jit(solution)/shard_map/reduce_scatter | solution.py:192
  109.9 6.1 %copy-start.1 = (pred[512,1024]{0,1:T(8,128)(4,1)}, pred[512,1024]{0,1:T(8,128)(4,1)S(1)}, u32[]{:S(2)}) copy-start(pred[512,1024]{0,1:T(8,128)(4,1)S(1)} %and_and_fusion.5) | copy-start | bytes 1572868 | tf_op jit(solution)/shard_map/while
  121.9 6.1 %copy-start.1 = (pred[512,1024]{0,1:T(8,128)(4,1)}, pred[512,1024]{0,1:T(8,128)(4,1)S(1)}, u32[]{:S(2)}) copy-start(pred[512,1024]{0,1:T(8,128)(4,1)S(1)} %and_and_fusion.5) | copy-start | bytes 1572868 | tf_op jit(solution)/shard_map/while
  134.2 6.0 %copy-start.1 = (pred[512,1024]{0,1:T(8,128)(4,1)}, pred[512,1024]{0,1:T(8,128)(4,1)S(1)}, u32[]{:S(2)}) copy-start(pred[512,1024]{0,1:T(8,128)(4,1)S(1)} %and_and_fusion.5) | copy-start | bytes 1572868 | tf_op jit(solution)/shard_map/while
  146.4 6.0 %copy-start.1 = (pred[512,1024]{0,1:T(8,128)(4,1)}, pred[512,1024]{0,1:T(8,128)(4,1)S(1)}, u32[]{:S(2)}) copy-start(pred[512,1024]{0,1:T(8,128)(4,1)S(1)} %and_and_fusion.5) | copy-start | bytes 1572868 | tf_op jit(solution)/shard_map/while
  159.4 2.7 %copy-start.3 = (f32[512,2,256]{2,0,1:T(8,128)S(1)}, f32[512,2,256]{2,0,1:T(8,128)}, u32[]{:S(2)}) copy-start(f32[512,2,256]{2,0,1:T(8,128)} %get-tuple-element.684) | copy-start | bytes 3145732 | tf_op jit(solution)/shard_map/while
  164.0 1.0 copy-start.4
  166.8 2.7 %copy-start.3 = (f32[512,2,256]{2,0,1:T(8,128)S(1)}, f32[512,2,256]{2,0,1:T(8,128)}, u32[]{:S(2)}) copy-start(f32[512,2,256]{2,0,1:T(8,128)} %get-tuple-element.684) | copy-start | bytes 3145732 | tf_op jit(solution)/shard_map/while
  171.4 1.0 copy-start.4
  177.7 58.6 %copy-start.2 = (bf16[128,2304]{1,0:T(8,128)(2,1)S(1)}, bf16[128,2304]{1,0:T(8,128)(2,1)}, u32[]{:S(2)}) copy-start(bf16[128,2304]{1,0:T(8,128)(2,1)} %param.16) | copy-start | bytes 1769476
  177.7 58.6 %copy-start.6 = (f32[2304]{0:T(1024)S(1)}, f32[2304]{0:T(1024)}, u32[]{:S(2)}) copy-start(f32[2304]{0:T(1024)} %param.18) | copy-start | bytes 27652
Sparse Core Ops, SparseCore 0:
  9.2 38.5 all-gather.9
  56.2 46.1 all-gather.11
  104.0 28.4 all-gather.13
  177.8 56.9 reduce-scatter.1
where the time goes:
time: 248 us; the launch traced here: 245 us
  waiting for transfers between devices  86.8 us (35%)
  matrix products  58.7 us (24%)
  blocking collectives  39.3 us (16%)
  local copies, waits for them, and re-layouts  26.4 us (11%)
  other arithmetic  19.3 us (8%)
  between operations  14 us (6%)
    reduce_scatter x1, waiting for transfers between devices, local(): lax.psum_scatter(jnp.dot(attended, out_weight, preferred_element_type=jnp...  57.1 us
    all_gather x1, waiting for transfers between devices, local(): portion = lax.all_gather(tokens, 'head', axis=0, tiled=True)  27.4 us
    dot_general x6, matrix products, advance(): jnp.einsum('qhk,kd->qhd', weights.astype(jnp.bfloat16), pair_rows[:, key_...  23.7 us
    dot_general x6, matrix products, advance(): jnp.einsum('qhd,kd->qhk', queries, pair_rows[:, :key_width], preferred_el...  23.6 us
    all_gather x1, blocking collectives, local(): lax.all_gather(segment_ids, 'seq', axis=0, tiled=True)  12.9 us
    all_gather x1, blocking collectives, local(): lax.all_gather(q_slot, 'seq', axis=0, tiled=True)  11.3 us
    unnamed x21, local copies, waits for them, and re-layouts  9.73 us
    squeeze x6, local copies, waits for them, and re-layouts, folding(): totals, _ = lax.scan(advance, totals, blocks)  8.59 us
  transfers between devices with their start and end apart: 4, of which 3 were waited for; matrix products, arithmetic and copies ran while one was open for 30% of the time, Pallas kernels for 0%

commit v1 on v0

v1 whole, which is shorter than its diff:
```python
import functools
import math

import jax
import jax.numpy as jnp
from jax import lax
from jax.experimental import pallas as pl
from jax.experimental.pallas import tpu as pltpu
from jax.sharding import PartitionSpec as P

QH = 8
KVH = 4
HD = 256
NSEG = 64
BLK = 16
LANES = 128
EPSILON = 1e-06
SOFT_CAP = 50.0
FAR = 1073741824
VMEM_BYTES = 40 << 20


def rms_scale(matrix, scaling):
    matrix = matrix.astype(jnp.float32)
    mean_square = jnp.mean(matrix * matrix, axis=-1, keepdims=True)
    return matrix * lax.rsqrt(mean_square + EPSILON) * scaling


def frequencies(extent):
    return 10000.0 ** (-(jnp.arange(extent // 2, dtype=jnp.float32) * 2.0 / extent))


def project_kernel(heads, which, x_ref, wq_ref, wkv_ref, cos_ref, sin_ref, q_ref, kv_ref):
    half = HD // 2
    x = x_ref[...]
    cosine, sine = cos_ref[...], sin_ref[...]
    for h in range(heads):
        y = jnp.dot(x, wq_ref[:, h * HD : (h + 1) * HD], preferred_element_type=jnp.float32)
        a, b = y[:, :half], y[:, half:]
        q_ref[h, :, :half] = ((a * cosine - b * sine) * HD**-0.5).astype(q_ref.dtype)
        q_ref[h, :, half:] = ((b * cosine + a * sine) * HD**-0.5).astype(q_ref.dtype)
    y = jnp.dot(x, wkv_ref[...], preferred_element_type=jnp.float32)
    a, b = y[:, :half], y[:, half:HD]
    kv_ref[:, :half] = (a * cosine - b * sine).astype(kv_ref.dtype)
    kv_ref[:, half:HD] = (b * cosine + a * sine).astype(kv_ref.dtype)
    kv_ref[:, HD:] = y[:, HD:].astype(kv_ref.dtype)


def project(normed, query_weight, keyval_weight, shared_head, cosine, sine):
    rows, width = normed.shape
    heads = query_weight.shape[1] // HD
    tile = math.gcd(rows, 256)
    return pl.pallas_call(
        functools.partial(project_kernel, heads),
        grid_spec=pltpu.PrefetchScalarGridSpec(
            num_scalar_prefetch=1,
            grid=(rows // tile,),
            in_specs=[
                pl.BlockSpec((tile, width), lambda i, s: (i, 0)),
                pl.BlockSpec((width, heads * HD), lambda i, s: (0, 0)),
                pl.BlockSpec((width, 2 * HD), lambda i, s: (0, s[0])),
                pl.BlockSpec((tile, HD // 2), lambda i, s: (i, 0)),
                pl.BlockSpec((tile, HD // 2), lambda i, s: (i, 0)),
            ],
            out_specs=[
                pl.BlockSpec((heads, tile, HD), lambda i, s: (0, i, 0)),
                pl.BlockSpec((tile, 2 * HD), lambda i, s: (i, 0)),
            ],
        ),
        out_shape=[
            jax.ShapeDtypeStruct((heads, rows, HD), jnp.bfloat16),
            jax.ShapeDtypeStruct((rows, 2 * HD), jnp.bfloat16),
        ],
        compiler_params=pltpu.CompilerParams(vmem_limit_bytes=VMEM_BYTES),
        cost_estimate=pl.CostEstimate(
            flops=2 * rows * width * (heads + 2) * HD,
            bytes_accessed=2 * width * (heads + 2) * HD + 2 * rows * width,
            transcendentals=0,
        ),
        name="project",
    )(shared_head.reshape(1), normed, query_weight, keyval_weight, cosine, sine)


def fold_blocks(
    heads, q_tile, k_tile, touch_ref, q_ref, qseg_ref, qslot_ref, kseg_ref, kslot_ref, parts, acc, den
):
    q_tiles = q_ref.shape[1] // q_tile
    blocks = kseg_ref.shape[0]
    first = 0
    for part in parts:
        here = part.shape[0] // k_tile

        def step(index, carry, part=part, here=here, first=first):
            qi = index // here
            kj = index % here

            @pl.when(touch_ref[qi * blocks + first + kj] > 0)
            def _():
                rows = pl.ds(pl.multiple_of(qi * q_tile, q_tile), q_tile)
                keys = pl.ds(pl.multiple_of(kj * k_tile, k_tile), k_tile)
                allowed = (kseg_ref[first + kj] == qseg_ref[rows, :]) & (
                    kslot_ref[first + kj] <= qslot_ref[rows, :]
                )
                for h in range(heads):
                    scores = lax.dot_general(
                        q_ref[h, rows, :],
                        part[keys, :HD],
                        (((1,), (1,)), ((), ())),
                        preferred_element_type=jnp.float32,
                    )
                    scores = jnp.tanh(scores * (1.0 / SOFT_CAP))
                    weights = jnp.where(
                        allowed, jnp.exp2(scores * (SOFT_CAP * math.log2(math.e))), 0.0
                    )
                    total = weights[:, :LANES]
                    for c in range(1, k_tile // LANES):
                        total += weights[:, c * LANES : (c + 1) * LANES]
                    den[h, rows, :] += total
                    acc[h, rows, :] += jnp.dot(
                        weights.astype(jnp.bfloat16),
                        part[keys, HD:],
                        preferred_element_type=jnp.float32,
                    )

            return carry

        lax.fori_loop(0, q_tiles * here, step, 0)
        first += here


def first_kernel(heads, q_tile, k_tile, count, touch_ref, q_ref, qseg_ref, qslot_ref, kseg_ref, kslot_ref, *rest):
    parts, (acc, den) = rest[:count], rest[count:]
    acc[...] = jnp.zeros_like(acc)
    den[...] = jnp.zeros_like(den)
    fold_blocks(
        heads, q_tile, k_tile, touch_ref, q_ref, qseg_ref, qslot_ref, kseg_ref, kslot_ref, parts, acc, den
    )


def last_kernel(heads, q_tile, k_tile, count, touch_ref, q_ref, qseg_ref, qslot_ref, kseg_ref, kslot_ref, *rest):
    parts, (acc_in, den_in, out_ref, acc, den) = rest[:count], rest[count:]
    acc[...] = acc_in[...]
    den[...] = den_in[...]
    fold_blocks(
        heads, q_tile, k_tile, touch_ref, q_ref, qseg_ref, qslot_ref, kseg_ref, kslot_ref, parts, acc, den
    )
    present = qseg_ref[...] >= 0
    for h in range(heads):
        total = jnp.sum(den[h], axis=-1, keepdims=True)
        safe = jnp.where(present, total, 1.0)
        out_ref[:, h * HD : (h + 1) * HD] = jnp.where(present, acc[h] / safe, 0.0).astype(
            out_ref.dtype
        )


def attend(queries, q_seg, q_slot, parts, k_seg, k_slot, totals=None):
    heads, rows, _ = queries.shape
    q_tile = math.gcd(rows, 256)
    k_tile = math.gcd(*[part.shape[0] for part in parts], 512)
    blocks = k_seg.shape[0] // k_tile
    seg_tiles = q_seg.reshape(-1, q_tile)
    lowest = jnp.min(jnp.where(seg_tiles >= 0, seg_tiles, FAR), axis=1)[:, None]
    highest = jnp.max(seg_tiles, axis=1)[:, None]
    latest = jnp.max(q_slot.reshape(-1, q_tile), axis=1)[:, None]
    near = (k_seg[None] >= lowest) & (k_seg[None] <= highest) & (k_slot[None] <= latest)
    touch = jnp.max(near.astype(jnp.int32).reshape(-1, blocks, k_tile), axis=2).reshape(-1)
    operands = [
        touch,
        queries,
        q_seg[:, None],
        q_slot[:, None],
        k_seg.reshape(blocks, 1, k_tile),
        k_slot.reshape(blocks, 1, k_tile),
        *parts,
    ]
    vmem = pl.BlockSpec(memory_space=pltpu.VMEM)
    sums = [
        jax.ShapeDtypeStruct((heads, rows, HD), jnp.float32),
        jax.ShapeDtypeStruct((heads, rows, LANES), jnp.float32),
    ]
    if totals is None:
        body, out_shape, out_specs, scratch = first_kernel, sums, [vmem, vmem], []
    else:
        operands += list(totals)
        body = last_kernel
        out_shape = jax.ShapeDtypeStruct((rows, heads * HD), jnp.bfloat16)
        out_specs = vmem
        scratch = [pltpu.VMEM(s.shape, s.dtype) for s in sums]
    pairs = heads * rows * k_seg.shape[0]
    return pl.pallas_call(
        functools.partial(body, heads, q_tile, k_tile, len(parts)),
        in_specs=[pl.BlockSpec(memory_space=pltpu.SMEM)] + [vmem] * (len(operands) - 1),
        out_specs=out_specs,
        out_shape=out_shape,
        scratch_shapes=scratch,
        compiler_params=pltpu.CompilerParams(vmem_limit_bytes=VMEM_BYTES),
        cost_estimate=pl.CostEstimate(
            flops=4 * pairs * HD, bytes_accessed=4 * HD * k_seg.shape[0], transcendentals=2 * pairs
        ),
        name="attend",
    )(*operands)


def local(
    tokens,
    in_gain,
    out_gain,
    query_weight,
    keyval_weight,
    out_weight,
    cache_entries,
    segment_ids,
    cache_lengths,
    block_owners,
):
    heads_here = query_weight.shape[1] // HD
    group_size = QH // KVH
    seq_size, head_size = lax.axis_size("seq"), lax.axis_size("head")
    seq_index = lax.axis_index("seq")
    head_index = lax.axis_index("head")
    shared_head = head_index * heads_here // group_size
    stream_rows = segment_ids.shape[0]
    own_rows = tokens.shape[0]
    square = head_size == 4

    def across(array, bits):
        return lax.ppermute(array, "head", [(h, h ^ bits) for h in range(head_size)])

    def relative(array):
        if not square:
            return array
        array = array.reshape(-1, 2, 2, own_rows)
        array = jnp.where(head_index % 2 == 1, array[:, :, ::-1], array)
        array = jnp.where(head_index // 2 == 1, array[:, ::-1], array)
        return array.reshape(-1)

    normed_own = rms_scale(tokens, in_gain).astype(jnp.bfloat16)
    if square:
        half = own_rows // 2
        from_x = across(normed_own, 1)
        from_y = across(normed_own, 2)
        diag_top = across(from_x[:half], 2)
        diag_bottom = across(from_y[half:], 1)
        normed = jnp.concatenate([normed_own, from_x, from_y, diag_top, diag_bottom], axis=0)
    else:
        normed = lax.all_gather(normed_own, "head", axis=0, tiled=True)

    cache_own = lax.dynamic_index_in_dim(cache_entries, shared_head, 0, keepdims=False)
    cache_pairs = lax.all_gather(cache_own, "seq", axis=0, tiled=True)

    table = lax.all_gather(jnp.concatenate([segment_ids, block_owners]), "seq", axis=0)
    seg_all = table[:, :stream_rows].reshape(-1)
    owners = table[:, stream_rows:].reshape(-1)

    seg_range = jnp.arange(NSEG, dtype=jnp.int32)
    earlier = (seg_all[None, :] >= 0) & (seg_all[None, :] < seg_range[:, None])
    firsts = jnp.sum(earlier.astype(jnp.int32), axis=1)
    slots_all = jnp.arange(seg_all.shape[0], dtype=jnp.int32)
    seg_all, slots_all = relative(seg_all), relative(slots_all)
    begin = seq_index * stream_rows
    q_seg = lax.dynamic_slice_in_dim(seg_all, begin, stream_rows)
    q_slot = lax.dynamic_slice_in_dim(slots_all, begin, stream_rows)
    matches = (q_seg[:, None] == seg_range[None, :]).astype(jnp.int32)
    positions = jnp.sum(matches * (cache_lengths - firsts)[None, :], axis=1) + q_slot
    angles = positions.astype(jnp.float32)[:, None] * frequencies(HD)[None, :]
    cosine, sine = jnp.cos(angles), jnp.sin(angles)

    block_index = jnp.arange(owners.shape[0], dtype=jnp.int32)
    same = (owners[:, None] == owners[None, :]) & (block_index[None, :] < block_index[:, None])
    block_rank = jnp.sum(same.astype(jnp.int32), axis=1)
    owner_match = (owners[:, None] == seg_range[None, :]).astype(jnp.int32)
    limits = jnp.sum(owner_match * cache_lengths[None, :], axis=1)
    offsets = jnp.arange(BLK, dtype=jnp.int32)
    usable = (owners[:, None] >= 0) & (
        block_rank[:, None] * BLK + offsets[None, :] < limits[:, None]
    )
    cache_seg = jnp.where(usable, owners[:, None], -2).reshape(-1)
    cache_slot = jnp.full((cache_seg.shape[0],), -1, jnp.int32)

    queries, pairs = project(normed, query_weight, keyval_weight, shared_head, cosine, sine)

    hops = seq_size // 4

    def onward(array):
        return lax.ppermute(array, "seq", [(s, s + 2) for s in range(seq_size - 2)])

    def sibling(array):
        return lax.ppermute(array, "seq", [(s, s ^ 1) for s in range(seq_size)])

    key_seg = jnp.where(seg_all >= 0, seg_all, -2)

    def shard_ints(shard):
        inside = (shard >= 0) & (shard < seq_size)
        at = jnp.clip(shard, 0, seq_size - 1) * stream_rows
        seg = lax.dynamic_slice_in_dim(key_seg, at, stream_rows)
        return jnp.where(inside, seg, -2), lax.dynamic_slice_in_dim(slots_all, at, stream_rows)

    mate = seq_index + 1 - 2 * (seq_index % 2)
    travelling = pairs
    far_parts, far_shards = [], []
    for hop in range(1, hops + 1):
        travelling = onward(travelling)
        far_parts += [travelling, sibling(travelling)]
        far_shards += [seq_index - 2 * hop, mate - 2 * hop]
    near_parts, near_shards = [pairs, sibling(pairs)], [seq_index, mate]

    near_ints = [shard_ints(s) for s in near_shards] + [(cache_seg, cache_slot)]
    far_ints = [shard_ints(s) for s in far_shards]
    totals = attend(
        queries,
        q_seg,
        q_slot,
        near_parts + [cache_pairs],
        jnp.concatenate([i[0] for i in near_ints]),
        jnp.concatenate([i[1] for i in near_ints]),
    )
    attended = attend(
        queries,
        q_seg,
        q_slot,
        far_parts,
        jnp.concatenate([i[0] for i in far_ints]),
        jnp.concatenate([i[1] for i in far_ints]),
        totals,
    )

    if square:
        r = own_rows
        c = out_weight.shape[1] // 2
        left = jnp.dot(attended, out_weight[:, :c], preferred_element_type=jnp.float32)
        right = jnp.dot(attended, out_weight[:, c:], preferred_element_type=jnp.float32)
        wire = jnp.bfloat16
        send_l = jnp.concatenate([left[r : 2 * r], left[3 * r :]]).astype(wire)
        got_l = across(send_l, 1).astype(jnp.float32)
        got_r = across(right[2 * r :].astype(wire), 2).astype(jnp.float32)
        last_l = across((left[2 * r : 3 * r] + got_l[r:]).astype(wire), 2)
        last_r = across((right[r : 2 * r] + got_r[r:]).astype(wire), 1)
        branch = jnp.concatenate(
            [
                left[:r] + got_l[:r] + last_l.astype(jnp.float32),
                right[:r] + got_r[:r] + last_r.astype(jnp.float32),
            ],
            axis=1,
        )
    else:
        branch = lax.psum_scatter(
            jnp.dot(attended, out_weight, preferred_element_type=jnp.float32),
            "head",
            scatter_dimension=0,
            tiled=True,
        )
    return (tokens.astype(jnp.float32) + rms_scale(branch, out_gain)).astype(jnp.bfloat16)


def solution(mesh):
    in_specs = (
        P(("seq", "head"), None),
        P(),
        P(),
        P(None, "head"),
        P(),
        P("head", None),
        P(None, "seq", None),
        P("seq"),
        P(),
        P("seq"),
    )
    out_specs = P(("seq", "head"), None)
    return jax.shard_map(local, mesh=mesh, in_specs=in_specs, out_specs=out_specs, check_vma=False)
```

time: 248 us -> 138 us (0.56)
  matrix products: 58.7 us -> 1.68 us
  waiting for transfers between devices: 86.8 us -> 46.9 us
  starting transfers between devices: 0.12 us -> 19.7 us
  blocking collectives: 39.3 us -> 22.2 us
  local copies, waits for them, and re-layouts: 26.4 us -> 10.3 us
  Pallas kernels: 0 us -> 12.3 us
  other arithmetic: 19.3 us -> 8.08 us
    reduce_scatter x1 -> x0, waiting for transfers between devices: 57.1 us -> none  [local(): lax.psum_scatter(jnp.dot(attended, out_weight, preferred_element_type=jnp...]
    dot_general x15 -> x2, matrix products: 58.7 us -> 1.68 us  [the longest x1 0.84 us: local(): jnp.dot(attended, out_weight[:, :c], preferred_element_type=jnp.float32)]
    ppermute x0 -> x13, waiting for transfers between devices: none -> 46.8 us  [the longest x8 26.8 us: across(): lax.ppermute(array, 'head', [(h, h ^ bits) for h in range(head_size)])]
    all_gather x3 -> x0, blocking collectives: 32.3 us -> none  [the longest x1 12.9 us: local(): lax.all_gather(segment_ids, 'seq', axis=0, tiled=True)]
    all_gather x3 -> x1, waiting for transfers between devices: 28.9 us -> 0.02 us  [local(): cache_pairs = lax.all_gather(cache_own, 'seq', axis=0, tiled=True)]
    ppermute x0 -> x13, starting transfers between devices: none -> 19.7 us  [the longest x2 10.2 us: onward(): return lax.ppermute(array, 'seq', [(s, s + 2) for s in range(seq_size - 2)])]
    unnamed x1, blocking collectives: 6.92 us -> 22.2 us
    pallas_call x0 -> x3, Pallas kernels: none -> 12.3 us  [the longest x2 7.13 us: attend(): pl.pallas_call(functools.partial(body, heads, q_tile, k_tile, len(parts))...]
  transfers between devices with their start and end apart: 4 -> 14, of which waited for: 3 -> 7; matrix products, arithmetic and copies ran while one was open for 30% -> 8% of each run, Pallas kernels for 0% -> 7%
where the time goes in v1:
time: 138 us; the launch traced here: 136 us
  waiting for transfers between devices  46.9 us (34%)
  blocking collectives  22.2 us (16%)
  starting transfers between devices  19.7 us (14%)
  between operations  14.7 us (11%)
  Pallas kernels  12.3 us (9%)
  local copies, waits for them, and re-layouts  10.3 us (7%)
  other arithmetic  8.08 us (6%)
  matrix products  1.68 us (1%)
    ppermute x8, waiting for transfers between devices, across(): lax.ppermute(array, 'head', [(h, h ^ bits) for h in range(head_size)])  26.8 us
    unnamed x1, blocking collectives  22.2 us
    ppermute x2, waiting for transfers between devices, onward(): return lax.ppermute(array, 'seq', [(s, s + 2) for s in range(seq_size - 2)])  20 us
    ppermute x2, starting transfers between devices, onward(): return lax.ppermute(array, 'seq', [(s, s + 2) for s in range(seq_size - 2)])  10.2 us
    ppermute x8, starting transfers between devices, across(): lax.ppermute(array, 'head', [(h, h ^ bits) for h in range(head_size)])  8.95 us
    pallas_call x2, Pallas kernels, attend(): pl.pallas_call(functools.partial(body, heads, q_tile, k_tile, len(parts))...  7.13 us
    unnamed x31, local copies, waits for them, and re-layouts  6.47 us
    pallas_call x1, Pallas kernels, project(): pl.pallas_call(functools.partial(project_kernel, heads), grid_spec=pltpu....  5.22 us
  transfers between devices with their start and end apart: 14, of which 7 were waited for; matrix products, arithmetic and copies ran while one was open for 8% of the time, Pallas kernels for 7%

profile of v1, /device:TPU:16, one launch (start us, length us, event | category | flops | bytes accessed | tf_op | source)
XLA Modules:
  0.0 135.8 jit_solution(3535568901685888417)
XLA Ops:
  6.5 1.4 fusion
  7.9 2.1 %constant_dynamic-update-slice_fusion.4 = (bf16[512,2304]{1,0:T(8,128)(2,1)S(1)}, bf16[128,2304]{1,0:T(8,128)(2,1)}) fusion(f32[2304]{0:T(1024)} %param.11, f32[128]{0:T(128)S(1)} %add_rsqrt_fusion.1, bf16[128,2304]{1,0:T(8,128)(2,1)} %param.10), kind=kLoop, calls=%fused_computation.53 | loop fusion | flops 1179647 | bytes 1779200
  10.1 1.5 %collective-permute-start = (bf16[128,2304]{1,0:T(8,128)(2,1)}, bf16[128,2304]{1,0:T(8,128)(2,1)}, u32[]{:S(2)}, u32[]{:S(2)}) collective-permute-start(bf16[128,2304]{1,0:T(8,128)(2,1)} %get-tuple-element.18), channel_id=1, source_target_pairs={{0,1},{1,0},{2,3},{3,2},{4,5},{5,4},{6,7},{7,6},{8,9},{9,8},{10,11... | collective-permute-start | bytes 1769480 | tf_op jit(solution)/shard_map/ppermute | solution.py:227
  11.6 1.5 %collective-permute-start.1 = (bf16[128,2304]{1,0:T(8,128)(2,1)}, bf16[128,2304]{1,0:T(8,128)(2,1)}, u32[]{:S(2)}, u32[]{:S(2)}) collective-permute-start(bf16[128,2304]{1,0:T(8,128)(2,1)} %get-tuple-element.18), channel_id=1, source_target_pairs={{0,2},{1,3},{2,0},{3,1},{4,6},{5,7},{6,4},{7,5},{8,10},{9,11},{10,... | collective-permute-start | bytes 1769480 | tf_op jit(solution)/shard_map/ppermute | solution.py:227
  13.1 0.7 constant_dynamic-slice_fusion
  13.9 0.6 dynamic-slice
  15.2 0.1 add_dynamic-update-slice_fusion
  15.3 22.2 %all-reduce = s32[4224]{0:T(1024)S(1)} all-reduce(s32[4224]{0:T(1024)S(1)} %add_dynamic-update-slice_fusion), channel_id=2, replica_groups=mesh['seq'=8,'head'=4] {'seq'}, use_global_device_ids=true, to_apply=%add | all-reduce | flops 4224 | bytes 33792
  37.5 0.1 reshape.213
  37.6 0.1 broadcast_in_dim_reshape.5
  37.7 0.2 convert_reduce_fusion.1
  38.0 0.2 convert_reduce_fusion
  38.3 0.1 select_reduce_fusion.1
  38.4 0.1 fusion.15
  38.7 0.1 select_n.162
  38.7 0.1 dynamic_slice.50
  38.8 0.1 select_reduce_fusion
  38.9 0.1 fusion.20
  39.0 1.0 multiply_sine_fusion
  40.0 1.0 slice.72
  41.0 0.3 collective-permute-start.2
  41.3 1.0 slice.73
  42.3 0.2 collective-permute-start.3
  42.5 1.1 constant_dynamic-update-slice_fusion.3
  43.6 1.3 constant_dynamic-update-slice_fusion.2
  44.8 5.7 %collective-permute-done.2 = bf16[64,2304]{1,0:T(8,128)(2,1)S(1)} collective-permute-done((bf16[64,2304]{1,0:T(8,128)(2,1)S(1)}, bf16[64,2304]{1,0:T(8,128)(2,1)S(1)}, u32[]{:S(2)}, u32[]{:S(2)}) %collective-permute-start.2) | collective-permute-done | bytes 294944 | tf_op jit(solution)/shard_map/ppermute | solution.py:227
  50.6 1.3 collective-permute-done.3
  52.0 5.2 %project.1 = (bf16[2,512,256]{2,1,0:T(8,128)(2,1)S(1)}, bf16[512,512]{1,0:T(8,128)(2,1)}) custom-call(s32[1]{0:T(128)} %bitcast.4.which, bf16[512,2304]{1,0:T(8,128)(2,1)S(1)} %constant_dynamic-update-slice_fusion.x_ref, bf16[2304,512]{1,0:T(8,128)(2,1)S(1)} %copy-done.1, bf16[2304,2048]{1,0:T(8,128)(2,1)} %wkv_ref.1, ...), custom_call_target="tpu_custom_call" | custom-call | flops 2415919104 | bytes 7077888 | tf_op jit(solution)/shard_map/project/pallas_call | solution.py:53
  57.2 0.8 copy-done.3
  58.0 5.7 %collective-permute-start.4 = (bf16[512,512]{1,0:T(8,128)(2,1)}, bf16[512,512]{1,0:T(8,128)(2,1)S(1)}, u32[]{:S(2)}, u32[]{:S(2)}) collective-permute-start(bf16[512,512]{1,0:T(8,128)(2,1)} %get-tuple-element.10.rest_0_), channel_id=1, source_target_pairs={{0,8},{4,12},{8,16},{12,20},{16,24},{20,28},{1,9},{5,13},{9,17},{1... | collective-permute-start | bytes 1572872 | tf_op jit(solution)/shard_map/ppermute | solution.py:285
  63.7 0.1 dynamic-slice_select_fusion.1
  63.9 0.1 reduce_max.36
  64.0 11.4 %collective-permute-done.4.rest_0_ = bf16[512,512]{1,0:T(8,128)(2,1)S(1)} collective-permute-done((bf16[512,512]{1,0:T(8,128)(2,1)}, bf16[512,512]{1,0:T(8,128)(2,1)S(1)}, u32[]{:S(2)}, u32[]{:S(2)}) %collective-permute-start.4) | collective-permute-done | bytes 524320 | tf_op jit(solution)/shard_map/ppermute | solution.py:285
  75.4 4.5 %collective-permute-start.6 = (bf16[512,512]{1,0:T(8,128)(2,1)S(1)}, bf16[512,512]{1,0:T(8,128)(2,1)S(1)}, u32[]{:S(2)}, u32[]{:S(2)}) collective-permute-start(bf16[512,512]{1,0:T(8,128)(2,1)S(1)} %collective-permute-done.4.rest_0_), channel_id=1, source_target_pairs={{0,8},{4,12},{8,16},{12,20},{16,24},{20,28},{1,9},{5,13},{9,17},{1... | collective-permute-start | bytes 1572872 | tf_op jit(solution)/shard_map/ppermute | solution.py:285
  79.8 0.1 fusion.17
  80.0 0.3 fusion.16
  80.3 0.1 copy.19
  80.3 0.1 reshape.210.touch_ref
  80.4 0.1 copy.23.qslot_ref
  80.6 0.1 copy.22.qseg_ref
  80.7 0.1 collective-permute-start.8
  80.9 0.2 convert_reduce_fusion.2
  81.1 0.1 reshape.208.touch_ref
  81.1 0.5 collective-permute-start.5
  81.6 8.6 %collective-permute-done.6.rest_2_ = bf16[512,512]{1,0:T(8,128)(2,1)S(1)} collective-permute-done((bf16[512,512]{1,0:T(8,128)(2,1)S(1)}, bf16[512,512]{1,0:T(8,128)(2,1)S(1)}, u32[]{:S(2)}, u32[]{:S(2)}) %collective-permute-start.6) | collective-permute-done | bytes 524320 | tf_op jit(solution)/shard_map/ppermute | solution.py:285
  90.3 1.6 %copy-done.2 = bf16[1,2048,512]{2,1,0:T(8,128)(2,1)S(1)} copy-done((bf16[1,2048,512]{2,1,0:T(8,128)(2,1)S(1)}, bf16[1,2048,512]{2,1,0:T(8,128)(2,1)}, u32[]{:S(2)}) %copy-start.2) | copy-done | bytes 2097176
  91.9 1.0 copy-done.4
  93.0 3.9 %attend.2 = (f32[2,512,256]{2,1,0:T(8,128)S(1)}, f32[2,512,128]{2,1,0:T(8,128)S(1)}) custom-call(s32[12]{0:T(128)S(1)} %reshape.210.touch_ref, bf16[2,512,256]{2,1,0:T(8,128)(2,1)S(1)} %copy-done.4, s32[512,1]{1,0:T(8,128)S(1)} %copy.22.qseg_ref, s32[512,1]{1,0:T(8,128)S(1)} %copy.23.qslot_ref, s32[6,1,512]{2,1,0:T(1,128)S(1)} %bitcast.23, ...), custom_call_target="tpu_custom_call" | custom-call | flops 3221225472 | bytes 3145728 | tf_op jit(solution)/shard_map/attend/pallas_call | solution.py:190
  96.9 3.3 %attend.3 = bf16[512,512]{1,0:T(8,128)(2,1)S(1)} custom-call(s32[8]{0:T(128)S(1)} %reshape.208.touch_ref, bf16[2,512,256]{2,1,0:T(8,128)(2,1)S(1)} %copy-done.4, s32[512,1]{1,0:T(8,128)S(1)} %copy.22.qseg_ref, s32[512,1]{1,0:T(8,128)S(1)} %copy.23.qslot_ref, s32[4,1,512]{2,1,0:T(1,128)S(1)} %pad_add_fusion.4.kseg_ref, ...), custom_call_target="tpu_custom_call" | custom-call | flops 2147483648 | bytes 2097152 | tf_op jit(solution)/shard_map/attend/pallas_call | solution.py:190
  100.2 0.8 fusion.21
  101.1 0.2 collective-permute-start.9
  101.3 0.8 fusion.4
  102.2 2.0 %collective-permute-start.11 = (bf16[256,1152]{1,0:T(8,128)(2,1)S(1)}, bf16[256,1152]{1,0:T(8,128)(2,1)S(1)}, u32[]{:S(2)}, u32[]{:S(2)}) collective-permute-start(bf16[256,1152]{1,0:T(8,128)(2,1)S(1)} %slice.108), channel_id=1, source_target_pairs={{0,2},{1,3},{2,0},{3,1},{4,6},{5,7},{6,4},{7,5},{8,10},{9,11},{10,... | collective-permute-start | bytes 1769480 | tf_op jit(solution)/shard_map/ppermute | solution.py:227
  104.3 12.3 %collective-permute-done.9 = bf16[256,1152]{1,0:T(8,128)(2,1)S(1)} collective-permute-done((bf16[256,1152]{1,0:T(8,128)(2,1)S(1)}, bf16[256,1152]{1,0:T(8,128)(2,1)S(1)}, u32[]{:S(2)}, u32[]{:S(2)}) %collective-permute-start.9) | collective-permute-done | bytes 589856 | tf_op jit(solution)/shard_map/ppermute | solution.py:227
  116.6 0.1 convert_element_type.56
  116.7 1.1 collective-permute-start.10
  117.9 0.1 convert_element_type.59
  118.0 2.1 %collective-permute-start.12 = (bf16[128,1152]{1,0:T(8,128)(2,1)S(1)}, bf16[128,1152]{1,0:T(8,128)(2,1)S(1)}, u32[]{:S(2)}, u32[]{:S(2)}) collective-permute-start(bf16[128,1152]{1,0:T(8,128)(2,1)S(1)} %fusion.9), channel_id=1, source_target_pairs={{0,1},{1,0},{2,3},{3,2},{4,5},{5,4},{6,7},{7,6},{8,9},{9,8},{10,11... | collective-permute-start | bytes 884744 | tf_op jit(solution)/shard_map/ppermute | solution.py:227
  120.1 6.5 %collective-permute-done.10 = bf16[128,1152]{1,0:T(8,128)(2,1)S(1)} collective-permute-done((bf16[128,1152]{1,0:T(8,128)(2,1)S(1)}, bf16[128,1152]{1,0:T(8,128)(2,1)S(1)}, u32[]{:S(2)}, u32[]{:S(2)}) %collective-permute-start.10) | collective-permute-done | bytes 294944 | tf_op jit(solution)/shard_map/ppermute | solution.py:227
  126.6 0.1 fusion.12
  126.7 0.9 collective-permute-done.12
  127.7 0.1 fusion.10
  127.7 0.2 multiply_reduce_fusion
  127.9 1.1 fusion.3
  (70 shorter events, 0.8 us)
Async XLA Ops:
  6.5 6.5 %copy-start = (bf16[4,256,512]{2,1,0:T(8,128)(2,1)S(1)}, bf16[4,256,512]{2,1,0:T(8,128)(2,1)}, u32[]{:S(2)}) copy-start(bf16[4,256,512]{2,1,0:T(8,128)(2,1)} %param.16) | copy-start | bytes 3145732
  6.5 83.8 %all-gather.4.cloned.1.call-start = ((), (), s32[]{:S(2)}) async-start(), calls=%async_computation | async-start | bytes 2359296 | tf_op jit(solution)/shard_map/all_gather | solution.py:249
  7.9 6.0 %copy-start.11 = (u32[32]{0:T(128)S(1)}, u32[32]{0:T(128)}, u32[]{:S(2)}) copy-start(u32[32]{0:T(128)} %constant.108) | copy-start | bytes 388
  7.9 7.2 %copy-start.8 = (s32[512]{0:T(512)S(1)}, s32[512]{0:T(512)}, u32[]{:S(2)}) copy-start(s32[512]{0:T(512)} %param.17) | copy-start | bytes 6148
  7.9 7.2 %copy-start.9 = (s32[16]{0:T(128)S(1)}, s32[16]{0:T(128)}, u32[]{:S(2)}) copy-start(s32[16]{0:T(128)} %param.19) | copy-start | bytes 196
  7.9 30.4 %copy-start.10 = (s32[64]{0:T(128)S(1)}, s32[64]{0:T(128)}, u32[]{:S(2)}) copy-start(s32[64]{0:T(128)} %param.18) | copy-start | bytes 772
  10.1 30.0 %collective-permute-start = (bf16[128,2304]{1,0:T(8,128)(2,1)}, bf16[128,2304]{1,0:T(8,128)(2,1)}, u32[]{:S(2)}, u32[]{:S(2)}) collective-permute-start(bf16[128,2304]{1,0:T(8,128)(2,1)} %get-tuple-element.18), channel_id=1, source_target_pairs={{0,1},{1,0},{2,3},{3,2},{4,5},{5,4},{6,7},{7,6},{8,9},{9,8},{10,11... | collective-permute-start | bytes 1769480 | tf_op jit(solution)/shard_map/ppermute | solution.py:227
  11.6 29.7 %collective-permute-start.1 = (bf16[128,2304]{1,0:T(8,128)(2,1)}, bf16[128,2304]{1,0:T(8,128)(2,1)}, u32[]{:S(2)}, u32[]{:S(2)}) collective-permute-start(bf16[128,2304]{1,0:T(8,128)(2,1)} %get-tuple-element.18), channel_id=1, source_target_pairs={{0,2},{1,3},{2,0},{3,1},{4,6},{5,7},{6,4},{7,5},{8,10},{9,11},{10,... | collective-permute-start | bytes 1769480 | tf_op jit(solution)/shard_map/ppermute | solution.py:227
  41.0 9.5 %collective-permute-start.2 = (bf16[64,2304]{1,0:T(8,128)(2,1)S(1)}, bf16[64,2304]{1,0:T(8,128)(2,1)S(1)}, u32[]{:S(2)}, u32[]{:S(2)}) collective-permute-start(bf16[64,2304]{1,0:T(8,128)(2,1)S(1)} %slice.72), channel_id=1, source_target_pairs={{0,2},{1,3},{2,0},{3,1},{4,6},{5,7},{6,4},{7,5},{8,10},{9,11},{10,... | collective-permute-start | bytes 884744 | tf_op jit(solution)/shard_map/ppermute | solution.py:227
  42.3 9.7 %collective-permute-start.3 = (bf16[64,2304]{1,0:T(8,128)(2,1)S(1)}, bf16[64,2304]{1,0:T(8,128)(2,1)S(1)}, u32[]{:S(2)}, u32[]{:S(2)}) collective-permute-start(bf16[64,2304]{1,0:T(8,128)(2,1)S(1)} %slice.73), channel_id=1, source_target_pairs={{0,1},{1,0},{2,3},{3,2},{4,5},{5,4},{6,7},{7,6},{8,9},{9,8},{10,11... | collective-permute-start | bytes 884744 | tf_op jit(solution)/shard_map/ppermute | solution.py:227
  43.6 8.4 %copy-start.1 = (bf16[2304,512]{1,0:T(8,128)(2,1)S(1)}, bf16[2304,512]{1,0:T(8,128)(2,1)}, u32[]{:S(2)}) copy-start(bf16[2304,512]{1,0:T(8,128)(2,1)} %wq_ref.1) | copy-start | bytes 7077892
  57.2 0.8 copy-start.3
  58.0 17.4 %collective-permute-start.4 = (bf16[512,512]{1,0:T(8,128)(2,1)}, bf16[512,512]{1,0:T(8,128)(2,1)S(1)}, u32[]{:S(2)}, u32[]{:S(2)}) collective-permute-start(bf16[512,512]{1,0:T(8,128)(2,1)} %get-tuple-element.10.rest_0_), channel_id=1, source_target_pairs={{0,8},{4,12},{8,16},{12,20},{16,24},{20,28},{1,9},{5,13},{9,17},{1... | collective-permute-start | bytes 1572872 | tf_op jit(solution)/shard_map/ppermute | solution.py:285
  75.4 14.9 %collective-permute-start.6 = (bf16[512,512]{1,0:T(8,128)(2,1)S(1)}, bf16[512,512]{1,0:T(8,128)(2,1)S(1)}, u32[]{:S(2)}, u32[]{:S(2)}) collective-permute-start(bf16[512,512]{1,0:T(8,128)(2,1)S(1)} %collective-permute-done.4.rest_0_), channel_id=1, source_target_pairs={{0,8},{4,12},{8,16},{12,20},{16,24},{20,28},{1,9},{5,13},{9,17},{1... | collective-permute-start | bytes 1572872 | tf_op jit(solution)/shard_map/ppermute | solution.py:285
  80.7 9.6 %collective-permute-start.8 = (bf16[512,512]{1,0:T(8,128)(2,1)}, bf16[512,512]{1,0:T(8,128)(2,1)S(1)}, u32[]{:S(2)}, u32[]{:S(2)}) collective-permute-start(bf16[512,512]{1,0:T(8,128)(2,1)} %get-tuple-element.10.rest_0_), channel_id=1, source_target_pairs={{0,4},{4,0},{8,12},{12,8},{16,20},{20,16},{24,28},{28,24},{1,5},{5... | collective-permute-start | bytes 1572872 | tf_op jit(solution)/shard_map/ppermute | solution.py:288
  81.1 15.7 %collective-permute-start.5 = (bf16[512,512]{1,0:T(8,128)(2,1)S(1)}, bf16[512,512]{1,0:T(8,128)(2,1)}, u32[]{:S(2)}, u32[]{:S(2)}) collective-permute-start(bf16[512,512]{1,0:T(8,128)(2,1)S(1)} %collective-permute-done.4.rest_0_), channel_id=1, source_target_pairs={{0,4},{4,0},{8,12},{12,8},{16,20},{20,16},{24,28},{28,24},{1,5},{5... | collective-permute-start | bytes 1572872 | tf_op jit(solution)/shard_map/ppermute | solution.py:288
  90.3 6.6 %collective-permute-start.7 = (bf16[512,512]{1,0:T(8,128)(2,1)S(1)}, bf16[512,512]{1,0:T(8,128)(2,1)}, u32[]{:S(2)}, u32[]{:S(2)}) collective-permute-start(bf16[512,512]{1,0:T(8,128)(2,1)S(1)} %collective-permute-done.6.rest_2_), channel_id=1, source_target_pairs={{0,4},{4,0},{8,12},{12,8},{16,20},{20,16},{24,28},{28,24},{1,5},{5... | collective-permute-start | bytes 1572872 | tf_op jit(solution)/shard_map/ppermute | solution.py:288
  90.3 1.6 %copy-start.2 = (bf16[1,2048,512]{2,1,0:T(8,128)(2,1)S(1)}, bf16[1,2048,512]{2,1,0:T(8,128)(2,1)}, u32[]{:S(2)}) copy-start(bf16[1,2048,512]{2,1,0:T(8,128)(2,1)} %all-gather.4.cloned.1.call-done) | copy-start | bytes 6291460
  91.9 1.0 copy-start.4
  96.9 3.3 %copy-start.6 = (bf16[512,2304]{1,0:T(8,128)(2,1)S(1)}, bf16[512,2304]{1,0:T(8,128)(2,1)}, u32[]{:S(2)}) copy-start(bf16[512,2304]{1,0:T(8,128)(2,1)} %param.15) | copy-start | bytes 7077892
  101.1 15.5 %collective-permute-start.9 = (bf16[256,1152]{1,0:T(8,128)(2,1)S(1)}, bf16[256,1152]{1,0:T(8,128)(2,1)S(1)}, u32[]{:S(2)}, u32[]{:S(2)}) collective-permute-start(bf16[256,1152]{1,0:T(8,128)(2,1)S(1)} %pad_maximum_fusion.1), channel_id=1, source_target_pairs={{0,1},{1,0},{2,3},{3,2},{4,5},{5,4},{6,7},{7,6},{8,9},{9,8},{10,11... | collective-permute-start | bytes 1769480 | tf_op jit(solution)/shard_map/ppermute | solution.py:227
  102.2 15.7 %collective-permute-start.11 = (bf16[256,1152]{1,0:T(8,128)(2,1)S(1)}, bf16[256,1152]{1,0:T(8,128)(2,1)S(1)}, u32[]{:S(2)}, u32[]{:S(2)}) collective-permute-start(bf16[256,1152]{1,0:T(8,128)(2,1)S(1)} %slice.108), channel_id=1, source_target_pairs={{0,2},{1,3},{2,0},{3,1},{4,6},{5,7},{6,4},{7,5},{8,10},{9,11},{10,... | collective-permute-start | bytes 1769480 | tf_op jit(solution)/shard_map/ppermute | solution.py:227
  116.7 9.9 %collective-permute-start.10 = (bf16[128,1152]{1,0:T(8,128)(2,1)S(1)}, bf16[128,1152]{1,0:T(8,128)(2,1)S(1)}, u32[]{:S(2)}, u32[]{:S(2)}) collective-permute-start(bf16[128,1152]{1,0:T(8,128)(2,1)S(1)} %fusion.11), channel_id=1, source_target_pairs={{0,2},{1,3},{2,0},{3,1},{4,6},{5,7},{6,4},{7,5},{8,10},{9,11},{10,... | collective-permute-start | bytes 884744 | tf_op jit(solution)/shard_map/ppermute | solution.py:227
  118.0 9.6 %collective-permute-start.12 = (bf16[128,1152]{1,0:T(8,128)(2,1)S(1)}, bf16[128,1152]{1,0:T(8,128)(2,1)S(1)}, u32[]{:S(2)}, u32[]{:S(2)}) collective-permute-start(bf16[128,1152]{1,0:T(8,128)(2,1)S(1)} %fusion.9), channel_id=1, source_target_pairs={{0,1},{1,0},{2,3},{3,2},{4,5},{5,4},{6,7},{7,6},{8,9},{9,8},{10,11... | collective-permute-start | bytes 884744 | tf_op jit(solution)/shard_map/ppermute | solution.py:227
  126.7 1.2 copy-start.5
  126.7 1.2 copy-start.7
Sparse Core Ops, SparseCore 0:
  13.9 28.2 all-gather.3

commit v2 on v1

--- a/solution.py
+++ b/solution.py
@@ -30,55 +30,57 @@
     return 10000.0 ** (-(jnp.arange(extent // 2, dtype=jnp.float32) * 2.0 / extent))
 
 
-def project_kernel(heads, which, x_ref, wq_ref, wkv_ref, cos_ref, sin_ref, q_ref, kv_ref):
+def turn(y, cosine, sine, scale):
+    half = y.shape[1] // 2
+    a, b = y[:, :half], y[:, half:]
+    return (a * cosine - b * sine) * scale, (b * cosine + a * sine) * scale
+
+
+def query_kernel(count, which_ref, cos_ref, sin_ref, w_ref, *rest):
+    parts, out_ref = rest[:count], rest[count]
     half = HD // 2
-    x = x_ref[...]
-    cosine, sine = cos_ref[...], sin_ref[...]
-    for h in range(heads):
-        y = jnp.dot(x, wq_ref[:, h * HD : (h + 1) * HD], preferred_element_type=jnp.float32)
-        a, b = y[:, :half], y[:, half:]
-        q_ref[h, :, :half] = ((a * cosine - b * sine) * HD**-0.5).astype(q_ref.dtype)
-        q_ref[h, :, half:] = ((b * cosine + a * sine) * HD**-0.5).astype(q_ref.dtype)
-    y = jnp.dot(x, wkv_ref[...], preferred_element_type=jnp.float32)
-    a, b = y[:, :half], y[:, half:HD]
-    kv_ref[:, :half] = (a * cosine - b * sine).astype(kv_ref.dtype)
-    kv_ref[:, half:HD] = (b * cosine + a * sine).astype(kv_ref.dtype)
-    kv_ref[:, HD:] = y[:, HD:].astype(kv_ref.dtype)
-
-
-def project(normed, query_weight, keyval_weight, shared_head, cosine, sine):
-    rows, width = normed.shape
-    heads = query_weight.shape[1] // HD
-    tile = math.gcd(rows, 256)
+    x = jnp.concatenate([part[...] for part in parts], axis=0)
+    for h in range(w_ref.shape[1] // HD):
+        y = jnp.dot(x, w_ref[:, h * HD : (h + 1) * HD], preferred_element_type=jnp.float32)
+        a, b = turn(y, cos_ref[...], sin_ref[...], HD**-0.5)
+        out_ref[h, :, :half] = a.astype(out_ref.dtype)
+        out_ref[h, :, half:] = b.astype(out_ref.dtype)
+
+
+def keyval_kernel(count, which_ref, cos_ref, sin_ref, w_ref, *rest):
+    parts, out_ref = rest[:count], rest[count]
+    half = HD // 2
+    x = jnp.concatenate([part[...] for part in parts], axis=0)
+    y = jnp.dot(x, w_ref[...], preferred_element_type=jnp.float32)
+    a, b = turn(y[:, :HD], cos_ref[...], sin_ref[...], 1.0)
+    out_ref[:, :half] = a.astype(out_ref.dtype)
+    out_ref[:, half:HD] = b.astype(out_ref.dtype)
+    out_ref[:, HD:] = y[:, HD:].astype(out_ref.dtype)
+
+
+def project(body, parts, weight, columns, which, cosine, sine, out_shape):
+    rows = cosine.shape[0]
+    width = weight.shape[0]
+    whole = [pl.BlockSpec(x.shape, lambda i, s: (0, 0)) for x in (cosine, sine)]
     return pl.pallas_call(
-        functools.partial(project_kernel, heads),
+        functools.partial(body, len(parts)),
         grid_spec=pltpu.PrefetchScalarGridSpec(
             num_scalar_prefetch=1,
-            grid=(rows // tile,),
-            in_specs=[
-                pl.BlockSpec((tile, width), lambda i, s: (i, 0)),
-                pl.BlockSpec((width, heads * HD), lambda i, s: (0, 0)),
-                pl.BlockSpec((width, 2 * HD), lambda i, s: (0, s[0])),
-                pl.BlockSpec((tile, HD // 2), lambda i, s: (i, 0)),
-                pl.BlockSpec((tile, HD // 2), lambda i, s: (i, 0)),
-            ],
-            out_specs=[
-                pl.BlockSpec((heads, tile, HD), lambda i, s: (0, i, 0)),
-                pl.BlockSpec((tile, 2 * HD), lambda i, s: (i, 0)),
-            ],
+            grid=(1,),
+            in_specs=whole
+            + [pl.BlockSpec((width, columns), lambda i, s: (0, s[0]))]
+            + [pl.BlockSpec(x.shape, lambda i, s: (0, 0)) for x in parts],
+            out_specs=pl.BlockSpec(out_shape, lambda i, s: (0,) * len(out_shape)),
         ),
-        out_shape=[
-            jax.ShapeDtypeStruct((heads, rows, HD), jnp.bfloat16),
-            jax.ShapeDtypeStruct((rows, 2 * HD), jnp.bfloat16),
-        ],
+        out_shape=jax.ShapeDtypeStruct(out_shape, jnp.bfloat16),
         compiler_params=pltpu.CompilerParams(vmem_limit_bytes=VMEM_BYTES),
         cost_estimate=pl.CostEstimate(
-            flops=2 * rows * width * (heads + 2) * HD,
-            bytes_accessed=2 * width * (heads + 2) * HD + 2 * rows * width,
+            flops=2 * rows * width * columns,
+            bytes_accessed=2 * width * (columns + rows),
             transcendentals=0,
         ),
         name="project",
-    )(shared_head.reshape(1), normed, query_weight, keyval_weight, cosine, sine)
+    )(which.reshape(1), cosine, sine, weight, *parts)
 
 
 def fold_blocks(
@@ -128,6 +130,15 @@
         first += here
 
 
+def middle_kernel(heads, q_tile, k_tile, count, touch_ref, q_ref, qseg_ref, qslot_ref, kseg_ref, kslot_ref, *rest):
+    parts, (acc_in, den_in, acc, den) = rest[:count], rest[count:]
+    acc[...] = acc_in[...]
+    den[...] = den_in[...]
+    fold_blocks(
+        heads, q_tile, k_tile, touch_ref, q_ref, qseg_ref, qslot_ref, kseg_ref, kslot_ref, parts, acc, den
+    )
+
+
 def first_kernel(heads, q_tile, k_tile, count, touch_ref, q_ref, qseg_ref, qslot_ref, kseg_ref, kslot_ref, *rest):
     parts, (acc, den) = rest[:count], rest[count:]
     acc[...] = jnp.zeros_like(acc)
@@ -153,8 +164,10 @@
         )
 
 
-def attend(queries, q_seg, q_slot, parts, k_seg, k_slot, totals=None):
+def attend(queries, q_seg, q_slot, parts, ints, totals=None, last=False):
     heads, rows, _ = queries.shape
+    k_seg = jnp.concatenate([pair[0] for pair in ints])
+    k_slot = jnp.concatenate([pair[1] for pair in ints])
     q_tile = math.gcd(rows, 256)
     k_tile = math.gcd(*[part.shape[0] for part in parts], 512)
     blocks = k_seg.shape[0] // k_tile
@@ -178,10 +191,11 @@
         jax.ShapeDtypeStruct((heads, rows, HD), jnp.float32),
         jax.ShapeDtypeStruct((heads, rows, LANES), jnp.float32),
     ]
-    if totals is None:
-        body, out_shape, out_specs, scratch = first_kernel, sums, [vmem, vmem], []
-    else:
+    body, out_shape, out_specs, scratch = first_kernel, sums, [vmem, vmem], []
+    if totals is not None:
         operands += list(totals)
+        body = middle_kernel
+    if last:
         body = last_kernel
         out_shape = jax.ShapeDtypeStruct((rows, heads * HD), jnp.bfloat16)
         out_specs = vmem
@@ -241,14 +255,24 @@
         from_y = across(normed_own, 2)
         diag_top = across(from_x[:half], 2)
         diag_bottom = across(from_y[half:], 1)
-        normed = jnp.concatenate([normed_own, from_x, from_y, diag_top, diag_bottom], axis=0)
+        chunks = [[normed_own, from_x], [from_y, diag_top, diag_bottom]]
     else:
-        normed = lax.all_gather(normed_own, "head", axis=0, tiled=True)
+        chunks = [[lax.all_gather(normed_own, "head", axis=0, tiled=True)]]
 
     cache_own = lax.dynamic_index_in_dim(cache_entries, shared_head, 0, keepdims=False)
     cache_pairs = lax.all_gather(cache_own, "seq", axis=0, tiled=True)
 
-    table = lax.all_gather(jnp.concatenate([segment_ids, block_owners]), "seq", axis=0)
+    table = jnp.concatenate([segment_ids, block_owners])[None]
+    bits = 0
+    while 1 << bits < seq_size:
+        step = 1 << bits
+        other = lax.ppermute(table, "seq", [(s, s ^ step) for s in range(seq_size)])
+        table = jnp.concatenate([table, other], axis=0)
+        bits += 1
+    for bit in range(bits):
+        pieces = table.reshape(-1, 2, 1 << bit, table.shape[-1])
+        pieces = jnp.where((seq_index >> bit) % 2 == 1, pieces[:, ::-1], pieces)
+        table = pieces.reshape(seq_size, -1)
     seg_all = table[:, :stream_rows].reshape(-1)
     owners = table[:, stream_rows:].reshape(-1)
 
@@ -277,7 +301,20 @@
     cache_seg = jnp.where(usable, owners[:, None], -2).reshape(-1)
     cache_slot = jnp.full((cache_seg.shape[0],), -1, jnp.int32)
 
-    queries, pairs = project(normed, query_weight, keyval_weight, shared_head, cosine, sine)
+    chunk_rows = stream_rows // len(chunks)
+    pairs = []
+    for at, parts in enumerate(chunks):
+        rows = slice(at * chunk_rows, (at + 1) * chunk_rows)
+        pairs.append(
+            project(
+                keyval_kernel, parts, keyval_weight, 2 * HD, shared_head,
+                cosine[rows], sine[rows], (chunk_rows, 2 * HD),
+            )
+        )
+    queries = project(
+        query_kernel, sum(chunks, []), query_weight, heads_here * HD, jnp.int32(0),
+        cosine, sine, (heads_here, stream_rows, HD),
+    )
 
     hops = seq_size // 4
 
@@ -296,33 +333,25 @@
         return jnp.where(inside, seg, -2), lax.dynamic_slice_in_dim(slots_all, at, stream_rows)
 
     mate = seq_index + 1 - 2 * (seq_index % 2)
-    travelling = pairs
-    far_parts, far_shards = [], []
+    travelling = [onward(pair) for pair in pairs]
+    waiting, waiting_ints = [sibling(pair) for pair in pairs], [shard_ints(mate)]
+    totals = attend(
+        queries, q_seg, q_slot, pairs + [cache_pairs], [shard_ints(seq_index), (cache_seg, cache_slot)]
+    )
     for hop in range(1, hops + 1):
-        travelling = onward(travelling)
-        far_parts += [travelling, sibling(travelling)]
-        far_shards += [seq_index - 2 * hop, mate - 2 * hop]
-    near_parts, near_shards = [pairs, sibling(pairs)], [seq_index, mate]
-
-    near_ints = [shard_ints(s) for s in near_shards] + [(cache_seg, cache_slot)]
-    far_ints = [shard_ints(s) for s in far_shards]
-    totals = attend(
-        queries,
-        q_seg,
-        q_slot,
-        near_parts + [cache_pairs],
-        jnp.concatenate([i[0] for i in near_ints]),
-        jnp.concatenate([i[1] for i in near_ints]),
-    )
-    attended = attend(
-        queries,
-        q_seg,
-        q_slot,
-        far_parts,
-        jnp.concatenate([i[0] for i in far_ints]),
-        jnp.concatenate([i[1] for i in far_ints]),
-        totals,
-    )
+        travelling, totals = lax.optimization_barrier((travelling, totals))
+        following = [onward(pair) for pair in travelling] if hop < hops else []
+        beside = [sibling(pair) for pair in travelling]
+        parts = waiting + travelling
+        ints = waiting_ints + [shard_ints(seq_index - 2 * hop)]
+        waiting, waiting_ints = beside, [shard_ints(mate - 2 * hop)]
+        if hop < hops:
+            totals = attend(queries, q_seg, q_slot, parts, ints, totals)
+        else:
+            attended = attend(
+                queries, q_seg, q_slot, parts + waiting, ints + waiting_ints, totals, last=True
+            )
+        travelling = following
 
     if square:
         r = own_rows

time: 138 us -> 128 us (0.928)
  blocking collectives: 22.2 us -> 0 us
  waiting for transfers between devices: 46.9 us -> 26.1 us
  local copies, waits for them, and re-layouts: 10.3 us -> 24.3 us
  starting transfers between devices: 19.7 us -> 31.9 us
  Pallas kernels: 12.3 us -> 20.7 us
    unnamed x1 -> x0, blocking collectives: 22.2 us -> none
    ppermute x2 -> x4, waiting for transfers between devices: 20 us -> 0.01 us  [onward(): return lax.ppermute(array, 'seq', [(s, s + 2) for s in range(seq_size - 2)])]
    unnamed x31 -> x86, local copies, waits for them, and re-layouts: 6.47 us -> 18.3 us
    ppermute x8, waiting for transfers between devices: 26.8 us -> 18.5 us  [across(): lax.ppermute(array, 'head', [(h, h ^ bits) for h in range(head_size)])]
    pallas_call x2 -> x3, Pallas kernels: 7.13 us -> 13.8 us  [attend(): pl.pallas_call(functools.partial(body, heads, q_tile, k_tile, len(parts))...]
    ppermute x0 -> x3, waiting for transfers between devices: none -> 6.53 us  [local(): other = lax.ppermute(table, 'seq', [(s, s ^ step) for s in range(seq_size)])]
    ppermute x2 -> x4, starting transfers between devices: 10.2 us -> 14.5 us  [onward(): return lax.ppermute(array, 'seq', [(s, s + 2) for s in range(seq_size - 2)])]
    ppermute x3 -> x6, starting transfers between devices: 0.56 us -> 3.7 us  [sibling(): return lax.ppermute(array, 'seq', [(s, s ^ 1) for s in range(seq_size)])]
  transfers between devices with their start and end apart: 14 -> 22, of which waited for: 7 -> 9; matrix products, arithmetic and copies ran while one was open for 8% -> 8% of each run, Pallas kernels for 7% -> 12%
where the time goes in v2:
time: 128 us; the launch traced here: 127 us
  starting transfers between devices  31.9 us (25%)
  waiting for transfers between devices  26.1 us (20%)
  local copies, waits for them, and re-layouts  24.3 us (19%)
  Pallas kernels  20.7 us (16%)
  between operations  14.2 us (11%)
  other arithmetic  8.03 us (6%)
  matrix products  1.68 us (1%)
    ppermute x8, waiting for transfers between devices, across(): lax.ppermute(array, 'head', [(h, h ^ bits) for h in range(head_size)])  18.5 us
    unnamed x86, local copies, waits for them, and re-layouts  18.3 us
    ppermute x4, starting transfers between devices, onward(): return lax.ppermute(array, 'seq', [(s, s + 2) for s in range(seq_size - 2)])  14.5 us
    pallas_call x3, Pallas kernels, attend(): pl.pallas_call(functools.partial(body, heads, q_tile, k_tile, len(parts))...  13.8 us
    ppermute x8, starting transfers between devices, across(): lax.ppermute(array, 'head', [(h, h ^ bits) for h in range(head_size)])  11.6 us
    pallas_call x3, Pallas kernels, project(): pl.pallas_call(functools.partial(body, len(parts)), grid_spec=pltpu.Prefe...  6.87 us
    ppermute x3, waiting for transfers between devices, local(): other = lax.ppermute(table, 'seq', [(s, s ^ step) for s in range(seq_size)])  6.53 us
    ppermute x6, starting transfers between devices, sibling(): return lax.ppermute(array, 'seq', [(s, s ^ 1) for s in range(seq_size)])  3.7 us
  transfers between devices with their start and end apart: 22, of which 9 were waited for; matrix products, arithmetic and copies ran while one was open for 8% of the time, Pallas kernels for 12%

profile of v2, /device:TPU:16, one launch (start us, length us, event | category | flops | bytes accessed | tf_op | source)
XLA Modules:
  0.0 126.9 jit_solution(780535973299569031)
XLA Ops:
  6.5 1.4 %fusion = f32[128]{0:T(128)S(1)} fusion(bf16[128,2304]{1,0:T(8,128)(2,1)} %param.10), kind=kLoop, calls=%fused_computation.3 | loop fusion | flops 884608 | bytes 590336 | tf_op jit(solution)/shard_map/reduce_sum | solution.py:25
  7.9 1.3 %fusion.2.rest_0_ = bf16[128,2304]{1,0:T(8,128)(2,1)S(1)} fusion(bf16[128,2304]{1,0:T(8,128)(2,1)} %param.10, f32[2304]{0:T(1024)} %param.11, f32[128]{0:T(128)S(1)} %add_rsqrt_fusion.1), kind=kLoop, calls=%fused_computation.5 | loop fusion | flops 1179648 | bytes 1189376 | tf_op jit(solution)/shard_map/convert_element_type | solution.py:251
  9.2 1.6 %collective-permute-start.3 = (bf16[128,2304]{1,0:T(8,128)(2,1)S(1)}, bf16[128,2304]{1,0:T(8,128)(2,1)S(1)}, u32[]{:S(2)}, u32[]{:S(2)}) collective-permute-start(bf16[128,2304]{1,0:T(8,128)(2,1)S(1)} %fusion.2.rest_0_), channel_id=1, source_target_pairs={{0,1},{1,0},{2,3},{3,2},{4,5},{5,4},{6,7},{7,6},{8,9},{9,8},{10,11... | collective-permute-start | bytes 1769480 | tf_op jit(solution)/shard_map/ppermute | solution.py:241
  10.8 1.5 %collective-permute-start.4 = (bf16[128,2304]{1,0:T(8,128)(2,1)S(1)}, bf16[128,2304]{1,0:T(8,128)(2,1)S(1)}, u32[]{:S(2)}, u32[]{:S(2)}) collective-permute-start(bf16[128,2304]{1,0:T(8,128)(2,1)S(1)} %fusion.2.rest_0_), channel_id=1, source_target_pairs={{0,2},{1,3},{2,0},{3,1},{4,6},{5,7},{6,4},{7,5},{8,10},{9,11},{10,... | collective-permute-start | bytes 1769480 | tf_op jit(solution)/shard_map/ppermute | solution.py:241
  12.4 0.7 constant_dynamic-slice_fusion
  13.2 0.4 collective-permute-done
  13.5 1.6 %collective-permute-start.1 = (s32[2,528]{1,0:T(2,128)S(1)}, s32[2,528]{1,0:T(2,128)S(1)}, u32[]{:S(2)}, u32[]{:S(2)}) collective-permute-start(s32[2,528]{1,0:T(2,128)S(1)} %pad_add_fusion.7), channel_id=1, source_target_pairs={{0,8},{4,12},{8,0},{12,4},{16,24},{20,28},{24,16},{28,20},{1,9},{5... | collective-permute-start | bytes 12680 | tf_op jit(solution)/shard_map/ppermute | solution.py:269
  15.2 2.0 %collective-permute-done.1 = s32[2,528]{1,0:T(2,128)S(1)} collective-permute-done((s32[2,528]{1,0:T(2,128)S(1)}, s32[2,528]{1,0:T(2,128)S(1)}, u32[]{:S(2)}, u32[]{:S(2)}) %collective-permute-start.1) | collective-permute-done | bytes 4256 | tf_op jit(solution)/shard_map/ppermute | solution.py:269
  17.2 0.4 collective-permute-start.2
  17.7 4.1 %collective-permute-done.2 = s32[4,528]{1,0:T(4,128)S(1)} collective-permute-done((s32[4,528]{1,0:T(4,128)S(1)}, s32[4,528]{1,0:T(4,128)S(1)}, u32[]{:S(2)}, u32[]{:S(2)}) %collective-permute-start.2) | collective-permute-done | bytes 8480 | tf_op jit(solution)/shard_map/ppermute | solution.py:269
  21.9 0.2 rev.21
  22.5 0.2 convert_reduce_fusion
  24.3 0.7 convert_reduce_fusion.2
  25.1 0.3 fusion.16
  25.4 1.0 multiply_sine_fusion
  26.4 0.7 fusion.20
  27.1 0.7 slice.88
  27.8 0.5 collective-permute-start.5
  28.3 0.7 slice.89
  29.1 0.5 collective-permute-start.6
  29.8 0.9 copy.28.qslot_ref
  30.7 0.8 copy.27.qseg_ref
  31.5 3.8 %copy-done.1 = bf16[2304,2048]{1,0:T(8,128)(2,1)S(1)} copy-done((bf16[2304,2048]{1,0:T(8,128)(2,1)S(1)}, bf16[2304,2048]{1,0:T(8,128)(2,1)}, u32[]{:S(2)}) %copy-start.1) | copy-done | bytes 9437208
  35.3 0.9 copy-done.4
  36.2 1.5 %project.4.rest_0_ = bf16[256,512]{1,0:T(8,128)(2,1)} custom-call(s32[1]{0:T(128)} %bitcast.12.which_ref, f32[256,128]{1,0:T(8,128)S(1)} %get-tuple-element.38.cos_ref, f32[256,128]{1,0:T(8,128)S(1)} %copy-done.4, bf16[2304,2048]{1,0:T(8,128)(2,1)S(1)} %copy-done.1, bf16[128,2304]{1,0:T(8,128)(2,1)S(1)} %fusion.2.rest_0_, ...), custom_call_target="tpu_custom_call" | custom-call | flops 603979776 | bytes 3538944 | tf_op jit(solution)/shard_map/project/pallas_call | solution.py:65
  37.7 3.7 %collective-permute-start.7 = (bf16[256,512]{1,0:T(8,128)(2,1)}, bf16[256,512]{1,0:T(8,128)(2,1)}, u32[]{:S(2)}, u32[]{:S(2)}) collective-permute-start(bf16[256,512]{1,0:T(8,128)(2,1)} %project.4.rest_0_), channel_id=1, source_target_pairs={{0,8},{4,12},{8,16},{12,20},{16,24},{20,28},{1,9},{5,13},{9,17},{1... | collective-permute-start | bytes 786440 | tf_op jit(solution)/shard_map/ppermute | solution.py:322
  41.6 2.9 %project.5.rest_1_ = bf16[256,512]{1,0:T(8,128)(2,1)} custom-call(s32[1]{0:T(128)} %bitcast.12.which_ref, f32[256,128]{1,0:T(8,128)S(1)} %get-tuple-element.37.cos_ref, f32[256,128]{1,0:T(8,128)S(1)} %get-tuple-element.35.sin_ref, bf16[2304,2048]{1,0:T(8,128)(2,1)S(1)} %copy-done.2, bf16[128,2304]{1,0:T(8,128)(2,1)S(1)} %collective-permute-done.4.rest_2_.rest_0_, ...), custom_call_target="tpu_custom_call" | custom-call | flops 603979776 | bytes 3538944 | tf_op jit(solution)/shard_map/project/pallas_call | solution.py:65
  44.5 1.9 %collective-permute-start.8 = (bf16[256,512]{1,0:T(8,128)(2,1)}, bf16[256,512]{1,0:T(8,128)(2,1)}, u32[]{:S(2)}, u32[]{:S(2)}) collective-permute-start(bf16[256,512]{1,0:T(8,128)(2,1)} %project.5.rest_1_), channel_id=1, source_target_pairs={{0,8},{4,12},{8,16},{12,20},{16,24},{20,28},{1,9},{5,13},{9,17},{1... | collective-permute-start | bytes 786440 | tf_op jit(solution)/shard_map/ppermute | solution.py:322
  46.4 0.5 collective-permute-start.14
  46.9 2.5 %project.3.q_ref = bf16[2,512,256]{2,1,0:T(8,128)(2,1)S(1)} custom-call(s32[1]{0:T(128)} %constant.112.clone.1.which_ref, f32[512,128]{1,0:T(8,128)S(1)} %get-tuple-element.56.cos_ref, f32[512,128]{1,0:T(8,128)S(1)} %get-tuple-element.55.sin_ref, bf16[2304,512]{1,0:T(8,128)(2,1)S(1)} %copy-done.3, bf16[128,2304]{1,0:T(8,128)(2,1)S(1)} %fusion.2.rest_0_, ...), custom_call_target="tpu_custom_call" | custom-call | flops 1207959552 | bytes 4718592 | tf_op jit(solution)/shard_map/project/pallas_call | solution.py:65
  49.4 0.8 copy-done.5
  50.2 1.0 copy-done.6
  51.2 0.9 copy-done.8
  52.2 0.9 copy-done.10
  53.2 1.6 %copy-done.12 = bf16[1,2048,512]{2,1,0:T(8,128)(2,1)S(1)} copy-done((bf16[1,2048,512]{2,1,0:T(8,128)(2,1)S(1)}, bf16[1,2048,512]{2,1,0:T(8,128)(2,1)}, u32[]{:S(2)}) %copy-start.12) | copy-done | bytes 2097176
  54.8 4.6 %attend.3 = (f32[2,512,256]{2,1,0:T(8,128)S(1)}, f32[2,512,128]{2,1,0:T(8,128)S(1)}) custom-call(s32[20]{0:T(128)S(1)} %reshape.267.touch_ref, bf16[2,512,256]{2,1,0:T(8,128)(2,1)S(1)} %copy-done.6, s32[512,1]{1,0:T(8,128)S(1)} %copy-done.10, s32[512,1]{1,0:T(8,128)S(1)} %copy-done.8, s32[10,1,256]{2,1,0:T(1,128)S(1)} %reshape.268.kseg_ref, ...), custom_call_target="tpu_custom_call" | custom-call | flops 2684354560 | bytes 2621440 | tf_op jit(solution)/shard_map/attend/pallas_call | solution.py:204
  59.4 1.0 copy-done.15
  60.4 0.8 copy-done.19
  61.2 6.8 %collective-permute-start.11 = (bf16[256,512]{1,0:T(8,128)(2,1)}, bf16[256,512]{1,0:T(8,128)(2,1)S(1)}, u32[]{:S(2)}, u32[]{:S(2)}) collective-permute-start(bf16[256,512]{1,0:T(8,128)(2,1)} %collective-permute-done.7.rest_2_), channel_id=1, source_target_pairs={{0,8},{4,12},{8,16},{12,20},{16,24},{20,28},{1,9},{5,13},{9,17},{1... | collective-permute-start | bytes 786440 | tf_op jit(solution)/shard_map/ppermute | solution.py:322
  68.0 2.1 %collective-permute-start.12 = (bf16[256,512]{1,0:T(8,128)(2,1)}, bf16[256,512]{1,0:T(8,128)(2,1)S(1)}, u32[]{:S(2)}, u32[]{:S(2)}) collective-permute-start(bf16[256,512]{1,0:T(8,128)(2,1)} %collective-permute-done.8.rest_3_), channel_id=1, source_target_pairs={{0,8},{4,12},{8,16},{12,20},{16,24},{20,28},{1,9},{5,13},{9,17},{1... | collective-permute-start | bytes 786440 | tf_op jit(solution)/shard_map/ppermute | solution.py:322
  70.4 0.5 collective-permute-start.9
  70.9 1.2 copy-done.16
  72.1 1.0 copy-done.20
  73.1 3.8 %attend.4 = (f32[2,512,256]{2,1,0:T(8,128)S(1)}, f32[2,512,128]{2,1,0:T(8,128)S(1)}) custom-call(s32[8]{0:T(128)S(1)} %reshape.270.touch_ref, bf16[2,512,256]{2,1,0:T(8,128)(2,1)S(1)} %copy-done.7, s32[512,1]{1,0:T(8,128)S(1)} %copy-done.11, s32[512,1]{1,0:T(8,128)S(1)} %copy-done.9, s32[4,1,256]{2,1,0:T(1,128)S(1)} %pad_add_fusion.11.kseg_ref, ...), custom_call_target="tpu_custom_call" | custom-call | flops 1073741824 | bytes 1048576 | tf_op jit(solution)/shard_map/attend/pallas_call | solution.py:204
  76.9 1.0 copy-done.13
  77.9 0.8 copy-done.17
  78.7 2.5 %collective-permute-start.15 = (bf16[256,512]{1,0:T(8,128)(2,1)S(1)}, bf16[256,512]{1,0:T(8,128)(2,1)S(1)}, u32[]{:S(2)}, u32[]{:S(2)}) collective-permute-start(bf16[256,512]{1,0:T(8,128)(2,1)S(1)} %collective-permute-done.11.rest_2_), channel_id=1, source_target_pairs={{0,4},{4,0},{8,12},{12,8},{16,20},{20,16},{24,28},{28,24},{1,5},{5... | collective-permute-start | bytes 786440 | tf_op jit(solution)/shard_map/ppermute | solution.py:325
  81.3 0.2 fusion.17
  81.7 0.6 collective-permute-done.15.rest_4_
  82.3 0.5 collective-permute-done.16.rest_5_
  82.9 1.2 copy-done.14
  84.1 1.0 copy-done.18
  85.1 5.4 %attend.5 = bf16[512,512]{1,0:T(8,128)(2,1)S(1)} custom-call(s32[12]{0:T(128)S(1)} %reshape.265.touch_ref, bf16[2,512,256]{2,1,0:T(8,128)(2,1)S(1)} %copy-done.7, s32[512,1]{1,0:T(8,128)S(1)} %copy-done.11, s32[512,1]{1,0:T(8,128)S(1)} %copy-done.9, s32[6,1,256]{2,1,0:T(1,128)S(1)} %pad_add_fusion.5.kseg_ref, s32[6,1,256]{2,1,0:T(1,128)S(1)} %pad_add_fusion.6.kslot_ref, ...), custom_call_target="tpu_custom_call" | custom-call | flops 1610612736 | bytes 1572864 | tf_op jit(solution)/shard_map/attend/pallas_call | solution.py:204
  90.6 0.8 fusion.23
  91.5 2.0 %collective-permute-start.17 = (bf16[256,1152]{1,0:T(8,128)(2,1)S(1)}, bf16[256,1152]{1,0:T(8,128)(2,1)S(1)}, u32[]{:S(2)}, u32[]{:S(2)}) collective-permute-start(bf16[256,1152]{1,0:T(8,128)(2,1)S(1)} %pad_maximum_fusion.1), channel_id=1, source_target_pairs={{0,1},{1,0},{2,3},{3,2},{4,5},{5,4},{6,7},{7,6},{8,9},{9,8},{10,11... | collective-permute-start | bytes 1769480 | tf_op jit(solution)/shard_map/ppermute | solution.py:241
  93.5 0.8 fusion.4
  94.4 2.1 %collective-permute-start.19 = (bf16[256,1152]{1,0:T(8,128)(2,1)S(1)}, bf16[256,1152]{1,0:T(8,128)(2,1)S(1)}, u32[]{:S(2)}, u32[]{:S(2)}) collective-permute-start(bf16[256,1152]{1,0:T(8,128)(2,1)S(1)} %slice.128), channel_id=1, source_target_pairs={{0,2},{1,3},{2,0},{3,1},{4,6},{5,7},{6,4},{7,5},{8,10},{9,11},{10,... | collective-permute-start | bytes 1769480 | tf_op jit(solution)/shard_map/ppermute | solution.py:241
  96.5 10.9 %collective-permute-done.17 = bf16[256,1152]{1,0:T(8,128)(2,1)S(1)} collective-permute-done((bf16[256,1152]{1,0:T(8,128)(2,1)S(1)}, bf16[256,1152]{1,0:T(8,128)(2,1)S(1)}, u32[]{:S(2)}, u32[]{:S(2)}) %collective-permute-start.17) | collective-permute-done | bytes 589856 | tf_op jit(solution)/shard_map/ppermute | solution.py:241
  107.5 2.1 %collective-permute-start.18 = (bf16[128,1152]{1,0:T(8,128)(2,1)S(1)}, bf16[128,1152]{1,0:T(8,128)(2,1)S(1)}, u32[]{:S(2)}, u32[]{:S(2)}) collective-permute-start(bf16[128,1152]{1,0:T(8,128)(2,1)S(1)} %fusion.11), channel_id=1, source_target_pairs={{0,2},{1,3},{2,0},{3,1},{4,6},{5,7},{6,4},{7,5},{8,10},{9,11},{10,... | collective-permute-start | bytes 884744 | tf_op jit(solution)/shard_map/ppermute | solution.py:241
  109.6 0.5 collective-permute-done.19
  110.2 1.3 %collective-permute-start.20 = (bf16[128,1152]{1,0:T(8,128)(2,1)S(1)}, bf16[128,1152]{1,0:T(8,128)(2,1)S(1)}, u32[]{:S(2)}, u32[]{:S(2)}) collective-permute-start(bf16[128,1152]{1,0:T(8,128)(2,1)S(1)} %fusion.9), channel_id=1, source_target_pairs={{0,1},{1,0},{2,3},{3,2},{4,5},{5,4},{6,7},{7,6},{8,9},{9,8},{10,11... | collective-permute-start | bytes 884744 | tf_op jit(solution)/shard_map/ppermute | solution.py:241
  111.5 5.0 %collective-permute-done.18 = bf16[128,1152]{1,0:T(8,128)(2,1)S(1)} collective-permute-done((bf16[128,1152]{1,0:T(8,128)(2,1)S(1)}, bf16[128,1152]{1,0:T(8,128)(2,1)S(1)}, u32[]{:S(2)}, u32[]{:S(2)}) %collective-permute-start.18) | collective-permute-done | bytes 294944 | tf_op jit(solution)/shard_map/ppermute | solution.py:241
  116.6 2.1 %collective-permute-done.20 = bf16[128,1152]{1,0:T(8,128)(2,1)S(1)} collective-permute-done((bf16[128,1152]{1,0:T(8,128)(2,1)S(1)}, bf16[128,1152]{1,0:T(8,128)(2,1)S(1)}, u32[]{:S(2)}, u32[]{:S(2)}) %collective-permute-start.20) | collective-permute-done | bytes 294944 | tf_op jit(solution)/shard_map/ppermute | solution.py:241
  119.0 1.1 fusion.3
  (170 shorter events, 3.6 us)
Async XLA Ops:
  6.5 5.9 %copy-start = (bf16[4,256,512]{2,1,0:T(8,128)(2,1)S(1)}, bf16[4,256,512]{2,1,0:T(8,128)(2,1)}, u32[]{:S(2)}) copy-start(bf16[4,256,512]{2,1,0:T(8,128)(2,1)} %param.16) | copy-start | bytes 3145732
  6.5 5.7 %copy-start.38 = (s32[512]{0:T(512)S(1)}, s32[512]{0:T(512)}, u32[]{:S(2)}) copy-start(s32[512]{0:T(512)} %param.17) | copy-start | bytes 6148
  6.5 5.7 %copy-start.40 = (s32[16]{0:T(128)S(1)}, s32[16]{0:T(128)}, u32[]{:S(2)}) copy-start(s32[16]{0:T(128)} %param.19) | copy-start | bytes 196
  6.5 43.7 %all-gather.3.cloned.1.call-start = ((), (), s32[]{:S(2)}) async-start(), calls=%async_computation | async-start | bytes 2359296 | tf_op jit(solution)/shard_map/all_gather | solution.py:263
  7.9 14.9 %copy-start.41 = (s32[64]{0:T(128)S(1)}, s32[64]{0:T(128)}, u32[]{:S(2)}) copy-start(s32[64]{0:T(128)} %param.18) | copy-start | bytes 772
  9.2 17.9 %collective-permute-start.3 = (bf16[128,2304]{1,0:T(8,128)(2,1)S(1)}, bf16[128,2304]{1,0:T(8,128)(2,1)S(1)}, u32[]{:S(2)}, u32[]{:S(2)}) collective-permute-start(bf16[128,2304]{1,0:T(8,128)(2,1)S(1)} %fusion.2.rest_0_), channel_id=1, source_target_pairs={{0,1},{1,0},{2,3},{3,2},{4,5},{5,4},{6,7},{7,6},{8,9},{9,8},{10,11... | collective-permute-start | bytes 1769480 | tf_op jit(solution)/shard_map/ppermute | solution.py:241
  10.8 17.6 %collective-permute-start.4 = (bf16[128,2304]{1,0:T(8,128)(2,1)S(1)}, bf16[128,2304]{1,0:T(8,128)(2,1)S(1)}, u32[]{:S(2)}, u32[]{:S(2)}) collective-permute-start(bf16[128,2304]{1,0:T(8,128)(2,1)S(1)} %fusion.2.rest_0_), channel_id=1, source_target_pairs={{0,2},{1,3},{2,0},{3,1},{4,6},{5,7},{6,4},{7,5},{8,10},{9,11},{10,... | collective-permute-start | bytes 1769480 | tf_op jit(solution)/shard_map/ppermute | solution.py:241
  12.3 1.2 collective-permute-start
  13.5 3.7 %collective-permute-start.1 = (s32[2,528]{1,0:T(2,128)S(1)}, s32[2,528]{1,0:T(2,128)S(1)}, u32[]{:S(2)}, u32[]{:S(2)}) collective-permute-start(s32[2,528]{1,0:T(2,128)S(1)} %pad_add_fusion.7), channel_id=1, source_target_pairs={{0,8},{4,12},{8,0},{12,4},{16,24},{20,28},{24,16},{28,20},{1,9},{5... | collective-permute-start | bytes 12680 | tf_op jit(solution)/shard_map/ppermute | solution.py:269
  17.2 4.6 %collective-permute-start.2 = (s32[4,528]{1,0:T(4,128)S(1)}, s32[4,528]{1,0:T(4,128)S(1)}, u32[]{:S(2)}, u32[]{:S(2)}) collective-permute-start(s32[4,528]{1,0:T(4,128)S(1)} %pad_add_fusion.2), channel_id=1, source_target_pairs={{0,16},{4,20},{8,24},{12,28},{16,0},{20,4},{24,8},{28,12},{1,17},{... | collective-permute-start | bytes 25352 | tf_op jit(solution)/shard_map/ppermute | solution.py:269
  23.6 1.5 %copy-start.23 = (s32[512]{0:T(512)}, s32[512]{0:T(512)S(1)}, u32[]{:S(2)}) copy-start(s32[512]{0:T(512)S(1)} %get-tuple-element.48) | copy-start | bytes 6148
  23.7 0.6 copy-start.27
  23.7 0.6 copy-start.29
  23.7 1.3 %copy-start.25 = (s32[512]{0:T(512)}, s32[512]{0:T(512)S(1)}, u32[]{:S(2)}) copy-start(s32[512]{0:T(512)S(1)} %get-tuple-element.44) | copy-start | bytes 6148
  23.9 2.5 %copy-start.32 = (s32[2]{0:T(128)}, s32[2]{0:T(128)S(1)}, u32[]{:S(2)}) copy-start(s32[2]{0:T(128)S(1)} %reduce_max.44) | copy-start | bytes 28
  24.1 2.3 %copy-start.34 = (s32[2]{0:T(128)}, s32[2]{0:T(128)S(1)}, u32[]{:S(2)}) copy-start(s32[2]{0:T(128)S(1)} %get-tuple-element.29) | copy-start | bytes 28
  24.1 2.3 %copy-start.36 = (s32[2]{0:T(128)}, s32[2]{0:T(128)S(1)}, u32[]{:S(2)}) copy-start(s32[2]{0:T(128)S(1)} %get-tuple-element.30) | copy-start | bytes 28
  27.8 13.7 %collective-permute-start.5 = (bf16[64,2304]{1,0:T(8,128)(2,1)}, bf16[64,2304]{1,0:T(8,128)(2,1)}, u32[]{:S(2)}, u32[]{:S(2)}) collective-permute-start(bf16[64,2304]{1,0:T(8,128)(2,1)} %slice.88), channel_id=1, source_target_pairs={{0,2},{1,3},{2,0},{3,1},{4,6},{5,7},{6,4},{7,5},{8,10},{9,11},{10,... | collective-permute-start | bytes 884744 | tf_op jit(solution)/shard_map/ppermute | solution.py:241
  29.1 12.5 %collective-permute-start.6 = (bf16[64,2304]{1,0:T(8,128)(2,1)}, bf16[64,2304]{1,0:T(8,128)(2,1)}, u32[]{:S(2)}, u32[]{:S(2)}) collective-permute-start(bf16[64,2304]{1,0:T(8,128)(2,1)} %slice.89), channel_id=1, source_target_pairs={{0,1},{1,0},{2,3},{3,2},{4,5},{5,4},{6,7},{7,6},{8,9},{9,8},{10,11... | collective-permute-start | bytes 884744 | tf_op jit(solution)/shard_map/ppermute | solution.py:241
  31.5 3.8 %copy-start.1 = (bf16[2304,2048]{1,0:T(8,128)(2,1)S(1)}, bf16[2304,2048]{1,0:T(8,128)(2,1)}, u32[]{:S(2)}) copy-start(bf16[2304,2048]{1,0:T(8,128)(2,1)} %w_ref.5) | copy-start | bytes 28311556
  35.3 0.9 copy-start.4
  36.2 5.4 %copy-start.2 = (bf16[2304,2048]{1,0:T(8,128)(2,1)S(1)}, bf16[2304,2048]{1,0:T(8,128)(2,1)}, u32[]{:S(2)}) copy-start(bf16[2304,2048]{1,0:T(8,128)(2,1)} %w_ref.5) | copy-start | bytes 28311556
  37.7 23.5 %collective-permute-start.7 = (bf16[256,512]{1,0:T(8,128)(2,1)}, bf16[256,512]{1,0:T(8,128)(2,1)}, u32[]{:S(2)}, u32[]{:S(2)}) collective-permute-start(bf16[256,512]{1,0:T(8,128)(2,1)} %project.4.rest_0_), channel_id=1, source_target_pairs={{0,8},{4,12},{8,16},{12,20},{16,24},{20,28},{1,9},{5,13},{9,17},{1... | collective-permute-start | bytes 786440 | tf_op jit(solution)/shard_map/ppermute | solution.py:322
  41.5 28.9 %collective-permute-start.13 = (bf16[256,512]{1,0:T(8,128)(2,1)}, bf16[256,512]{1,0:T(8,128)(2,1)}, u32[]{:S(2)}, u32[]{:S(2)}) collective-permute-start(bf16[256,512]{1,0:T(8,128)(2,1)} %project.4.rest_0_), channel_id=1, source_target_pairs={{0,4},{4,0},{8,12},{12,8},{16,20},{20,16},{24,28},{28,24},{1,5},{5... | collective-permute-start | bytes 786440 | tf_op jit(solution)/shard_map/ppermute | solution.py:325
  41.6 5.3 %copy-start.3 = (bf16[2304,512]{1,0:T(8,128)(2,1)S(1)}, bf16[2304,512]{1,0:T(8,128)(2,1)}, u32[]{:S(2)}) copy-start(bf16[2304,512]{1,0:T(8,128)(2,1)} %w_ref.3) | copy-start | bytes 7077892
  44.5 16.7 %collective-permute-start.8 = (bf16[256,512]{1,0:T(8,128)(2,1)}, bf16[256,512]{1,0:T(8,128)(2,1)}, u32[]{:S(2)}, u32[]{:S(2)}) collective-permute-start(bf16[256,512]{1,0:T(8,128)(2,1)} %project.5.rest_1_), channel_id=1, source_target_pairs={{0,8},{4,12},{8,16},{12,20},{16,24},{20,28},{1,9},{5,13},{9,17},{1... | collective-permute-start | bytes 786440 | tf_op jit(solution)/shard_map/ppermute | solution.py:322
  46.4 24.5 %collective-permute-start.14 = (bf16[256,512]{1,0:T(8,128)(2,1)}, bf16[256,512]{1,0:T(8,128)(2,1)}, u32[]{:S(2)}, u32[]{:S(2)}) collective-permute-start(bf16[256,512]{1,0:T(8,128)(2,1)} %project.5.rest_1_), channel_id=1, source_target_pairs={{0,4},{4,0},{8,12},{12,8},{16,20},{20,16},{24,28},{28,24},{1,5},{5... | collective-permute-start | bytes 786440 | tf_op jit(solution)/shard_map/ppermute | solution.py:325
  49.4 0.8 copy-start.5
  50.2 1.0 copy-start.6
  51.2 0.9 copy-start.8
  52.2 0.9 copy-start.10
  53.1 1.6 %copy-start.12 = (bf16[1,2048,512]{2,1,0:T(8,128)(2,1)S(1)}, bf16[1,2048,512]{2,1,0:T(8,128)(2,1)}, u32[]{:S(2)}) copy-start(bf16[1,2048,512]{2,1,0:T(8,128)(2,1)} %all-gather.3.cloned.1.call-done) | copy-start | bytes 6291460
  54.7 15.3 %copy-start.24 = (s32[512]{0:T(512)S(1)}, s32[512]{0:T(512)}, u32[]{:S(2)}) copy-start(s32[512]{0:T(512)} %copy-done.23) | copy-start | bytes 6148
  54.7 15.4 %copy-start.39 = (s32[2,4]{1,0:T(2,128)S(1)}, s32[2,4]{1,0:T(2,128)}, u32[]{:S(2)}) copy-start(s32[2,4]{1,0:T(2,128)} %convert_reduce_fusion.2) | copy-start | bytes 100
  54.7 16.1 %copy-start.7 = (bf16[2,512,256]{2,1,0:T(8,128)(2,1)S(1)}, bf16[2,512,256]{2,1,0:T(8,128)(2,1)}, u32[]{:S(2)}) copy-start(bf16[2,512,256]{2,1,0:T(8,128)(2,1)} %copy-done.5) | copy-start | bytes 1572868
  54.7 16.1 %copy-start.9 = (s32[512,1]{1,0:T(8,128)S(1)}, s32[512,1]{1,0:T(8,128)}, u32[]{:S(2)}) copy-start(s32[512,1]{1,0:T(8,128)} %copy.28.qslot_ref) | copy-start | bytes 6148
  54.8 16.1 %copy-start.11 = (s32[512,1]{1,0:T(8,128)S(1)}, s32[512,1]{1,0:T(8,128)}, u32[]{:S(2)}) copy-start(s32[512,1]{1,0:T(8,128)} %copy.27.qseg_ref) | copy-start | bytes 6148
  59.4 1.0 copy-start.15
  60.4 0.8 copy-start.19
  61.2 17.5 %collective-permute-start.11 = (bf16[256,512]{1,0:T(8,128)(2,1)}, bf16[256,512]{1,0:T(8,128)(2,1)S(1)}, u32[]{:S(2)}, u32[]{:S(2)}) collective-permute-start(bf16[256,512]{1,0:T(8,128)(2,1)} %collective-permute-done.7.rest_2_), channel_id=1, source_target_pairs={{0,8},{4,12},{8,16},{12,20},{16,24},{20,28},{1,9},{5,13},{9,17},{1... | collective-permute-start | bytes 786440 | tf_op jit(solution)/shard_map/ppermute | solution.py:322
  68.0 10.8 %collective-permute-start.12 = (bf16[256,512]{1,0:T(8,128)(2,1)}, bf16[256,512]{1,0:T(8,128)(2,1)S(1)}, u32[]{:S(2)}, u32[]{:S(2)}) collective-permute-start(bf16[256,512]{1,0:T(8,128)(2,1)} %collective-permute-done.8.rest_3_), channel_id=1, source_target_pairs={{0,8},{4,12},{8,16},{12,20},{16,24},{20,28},{1,9},{5,13},{9,17},{1... | collective-permute-start | bytes 786440 | tf_op jit(solution)/shard_map/ppermute | solution.py:322
  70.2 11.0 %copy-start.33 = (s32[2]{0:T(128)S(1)}, s32[2]{0:T(128)}, u32[]{:S(2)}) copy-start(s32[2]{0:T(128)} %copy-done.32) | copy-start | bytes 28
  70.2 11.0 %copy-start.35 = (s32[2]{0:T(128)S(1)}, s32[2]{0:T(128)}, u32[]{:S(2)}) copy-start(s32[2]{0:T(128)} %copy-done.34) | copy-start | bytes 28
  70.2 11.0 %copy-start.37 = (s32[2]{0:T(128)S(1)}, s32[2]{0:T(128)}, u32[]{:S(2)}) copy-start(s32[2]{0:T(128)} %copy-done.36) | copy-start | bytes 28
  70.2 11.5 %copy-start.26 = (s32[512]{0:T(512)S(1)}, s32[512]{0:T(512)}, u32[]{:S(2)}) copy-start(s32[512]{0:T(512)} %copy-done.25) | copy-start | bytes 6148
  70.2 11.5 %copy-start.28 = (s32[512]{0:T(512)S(1)}, s32[512]{0:T(512)}, u32[]{:S(2)}) copy-start(s32[512]{0:T(512)} %copy-done.27) | copy-start | bytes 6148
  70.3 11.4 %copy-start.30 = (s32[512]{0:T(512)S(1)}, s32[512]{0:T(512)}, u32[]{:S(2)}) copy-start(s32[512]{0:T(512)} %copy-done.29) | copy-start | bytes 6148
  70.3 11.5 %collective-permute-start.10 = (bf16[256,512]{1,0:T(8,128)(2,1)}, bf16[256,512]{1,0:T(8,128)(2,1)S(1)}, u32[]{:S(2)}, u32[]{:S(2)}) collective-permute-start(bf16[256,512]{1,0:T(8,128)(2,1)} %collective-permute-done.8.rest_3_), channel_id=1, source_target_pairs={{0,4},{4,0},{8,12},{12,8},{16,20},{20,16},{24,28},{28,24},{1,5},{5... | collective-permute-start | bytes 786440 | tf_op jit(solution)/shard_map/ppermute | solution.py:325
  70.4 11.4 %collective-permute-start.9 = (bf16[256,512]{1,0:T(8,128)(2,1)}, bf16[256,512]{1,0:T(8,128)(2,1)S(1)}, u32[]{:S(2)}, u32[]{:S(2)}) collective-permute-start(bf16[256,512]{1,0:T(8,128)(2,1)} %collective-permute-done.7.rest_2_), channel_id=1, source_target_pairs={{0,4},{4,0},{8,12},{12,8},{16,20},{20,16},{24,28},{28,24},{1,5},{5... | collective-permute-start | bytes 786440 | tf_op jit(solution)/shard_map/ppermute | solution.py:325
  70.9 1.2 copy-start.16
  72.1 1.0 copy-start.20
  76.9 1.0 copy-start.13
  77.9 0.8 copy-start.17
  78.7 3.6 %collective-permute-start.15 = (bf16[256,512]{1,0:T(8,128)(2,1)S(1)}, bf16[256,512]{1,0:T(8,128)(2,1)S(1)}, u32[]{:S(2)}, u32[]{:S(2)}) collective-permute-start(bf16[256,512]{1,0:T(8,128)(2,1)S(1)} %collective-permute-done.11.rest_2_), channel_id=1, source_target_pairs={{0,4},{4,0},{8,12},{12,8},{16,20},{20,16},{24,28},{28,24},{1,5},{5... | collective-permute-start | bytes 786440 | tf_op jit(solution)/shard_map/ppermute | solution.py:325
  81.2 1.7 %collective-permute-start.16 = (bf16[256,512]{1,0:T(8,128)(2,1)S(1)}, bf16[256,512]{1,0:T(8,128)(2,1)}, u32[]{:S(2)}, u32[]{:S(2)}) collective-permute-start(bf16[256,512]{1,0:T(8,128)(2,1)S(1)} %collective-permute-done.12.rest_3_), channel_id=1, source_target_pairs={{0,4},{4,0},{8,12},{12,8},{16,20},{20,16},{24,28},{28,24},{1,5},{5... | collective-permute-start | bytes 786440 | tf_op jit(solution)/shard_map/ppermute | solution.py:325
  82.9 1.2 copy-start.14
  84.1 1.0 copy-start.18
  85.1 5.4 %copy-start.22 = (bf16[512,2304]{1,0:T(8,128)(2,1)S(1)}, bf16[512,2304]{1,0:T(8,128)(2,1)}, u32[]{:S(2)}) copy-start(bf16[512,2304]{1,0:T(8,128)(2,1)} %param.15) | copy-start | bytes 7077892
  91.5 15.8 %collective-permute-start.17 = (bf16[256,1152]{1,0:T(8,128)(2,1)S(1)}, bf16[256,1152]{1,0:T(8,128)(2,1)S(1)}, u32[]{:S(2)}, u32[]{:S(2)}) collective-permute-start(bf16[256,1152]{1,0:T(8,128)(2,1)S(1)} %pad_maximum_fusion.1), channel_id=1, source_target_pairs={{0,1},{1,0},{2,3},{3,2},{4,5},{5,4},{6,7},{7,6},{8,9},{9,8},{10,11... | collective-permute-start | bytes 1769480 | tf_op jit(solution)/shard_map/ppermute | solution.py:241
  94.4 15.7 %collective-permute-start.19 = (bf16[256,1152]{1,0:T(8,128)(2,1)S(1)}, bf16[256,1152]{1,0:T(8,128)(2,1)S(1)}, u32[]{:S(2)}, u32[]{:S(2)}) collective-permute-start(bf16[256,1152]{1,0:T(8,128)(2,1)S(1)} %slice.128), channel_id=1, source_target_pairs={{0,2},{1,3},{2,0},{3,1},{4,6},{5,7},{6,4},{7,5},{8,10},{9,11},{10,... | collective-permute-start | bytes 1769480 | tf_op jit(solution)/shard_map/ppermute | solution.py:241
  107.5 9.0 %collective-permute-start.18 = (bf16[128,1152]{1,0:T(8,128)(2,1)S(1)}, bf16[128,1152]{1,0:T(8,128)(2,1)S(1)}, u32[]{:S(2)}, u32[]{:S(2)}) collective-permute-start(bf16[128,1152]{1,0:T(8,128)(2,1)S(1)} %fusion.11), channel_id=1, source_target_pairs={{0,2},{1,3},{2,0},{3,1},{4,6},{5,7},{6,4},{7,5},{8,10},{9,11},{10,... | collective-permute-start | bytes 884744 | tf_op jit(solution)/shard_map/ppermute | solution.py:241
  110.2 8.5 %collective-permute-start.20 = (bf16[128,1152]{1,0:T(8,128)(2,1)S(1)}, bf16[128,1152]{1,0:T(8,128)(2,1)S(1)}, u32[]{:S(2)}, u32[]{:S(2)}) collective-permute-start(bf16[128,1152]{1,0:T(8,128)(2,1)S(1)} %fusion.9), channel_id=1, source_target_pairs={{0,1},{1,0},{2,3},{3,2},{4,5},{5,4},{6,7},{7,6},{8,9},{9,8},{10,11... | collective-permute-start | bytes 884744 | tf_op jit(solution)/shard_map/ppermute | solution.py:241
  116.6 2.4 %copy-start.21 = (bf16[128,2304]{1,0:T(8,128)(2,1)S(1)}, bf16[128,2304]{1,0:T(8,128)(2,1)}, u32[]{:S(2)}) copy-start(bf16[128,2304]{1,0:T(8,128)(2,1)} %param.10) | copy-start | bytes 1769476
  116.6 2.4 %copy-start.31 = (f32[2304]{0:T(1024)S(1)}, f32[2304]{0:T(1024)}, u32[]{:S(2)}) copy-start(f32[2304]{0:T(1024)} %param.12) | copy-start | bytes 27652
Sparse Core Ops, SparseCore 0:
  13.3 27.8 all-gather.2

commit v3 on v2

--- a/solution.py
+++ b/solution.py
@@ -301,13 +301,14 @@
     cache_seg = jnp.where(usable, owners[:, None], -2).reshape(-1)
     cache_slot = jnp.full((cache_seg.shape[0],), -1, jnp.int32)
 
+    w_shared = lax.dynamic_slice_in_dim(keyval_weight, shared_head * 2 * HD, 2 * HD, 1)
     chunk_rows = stream_rows // len(chunks)
     pairs = []
     for at, parts in enumerate(chunks):
         rows = slice(at * chunk_rows, (at + 1) * chunk_rows)
         pairs.append(
             project(
-                keyval_kernel, parts, keyval_weight, 2 * HD, shared_head,
+                keyval_kernel, parts, w_shared, 2 * HD, jnp.int32(0),
                 cosine[rows], sine[rows], (chunk_rows, 2 * HD),
             )
         )

time: 128 us -> 148 us (1.16)
  local copies, waits for them, and re-layouts: 24.3 us -> 40.1 us
  Pallas kernels: 20.7 us -> 26 us
  waiting for transfers between devices: 26.1 us -> 20.9 us
  other arithmetic: 8.03 us -> 11.4 us
    unnamed x86 -> x124, local copies, waits for them, and re-layouts: 18.3 us -> 23.7 us
    ppermute x8, waiting for transfers between devices: 18.5 us -> 13.7 us  [across(): lax.ppermute(array, 'head', [(h, h ^ bits) for h in range(head_size)])]
    pallas_call x3, Pallas kernels: 13.8 us -> 17.4 us  [attend(): pl.pallas_call(functools.partial(body, heads, q_tile, k_tile, len(parts))...]
    dynamic_slice x0 -> x1, local copies, waits for them, and re-layouts: none -> 1.82 us  [local(): lax.dynamic_slice_in_dim(keyval_weight, shared_head * 2 * HD, 2 * HD, 1)]
    pallas_call x3, Pallas kernels: 6.87 us -> 8.59 us  [project(): pl.pallas_call(functools.partial(body, len(parts)), grid_spec=pltpu.Prefe...]
    ppermute x4, starting transfers between devices: 14.5 us -> 13 us  [onward(): return lax.ppermute(array, 'seq', [(s, s + 2) for s in range(seq_size - 2)])]
  transfers between devices with their start and end apart: 22 -> 22, of which waited for: 9 -> 7; matrix products, arithmetic and copies ran while one was open for 8% -> 16% of each run, Pallas kernels for 12% -> 12%
where the time goes in v3:
time: 148 us; the launch traced here: 146 us
  local copies, waits for them, and re-layouts  40.1 us (27%)
  starting transfers between devices  31.5 us (21%)
  Pallas kernels  26 us (18%)
  waiting for transfers between devices  20.9 us (14%)
  between operations  14.2 us (10%)
  other arithmetic  11.4 us (8%)
  matrix products  1.69 us (1%)
    unnamed x124, local copies, waits for them, and re-layouts  23.7 us
    pallas_call x3, Pallas kernels, attend(): pl.pallas_call(functools.partial(body, heads, q_tile, k_tile, len(parts))...  17.4 us
    ppermute x8, waiting for transfers between devices, across(): lax.ppermute(array, 'head', [(h, h ^ bits) for h in range(head_size)])  13.7 us
    ppermute x4, starting transfers between devices, onward(): return lax.ppermute(array, 'seq', [(s, s + 2) for s in range(seq_size - 2)])  13 us
    ppermute x8, starting transfers between devices, across(): lax.ppermute(array, 'head', [(h, h ^ bits) for h in range(head_size)])  11.4 us
    pallas_call x3, Pallas kernels, project(): pl.pallas_call(functools.partial(body, len(parts)), grid_spec=pltpu.Prefe...  8.59 us
    ppermute x3, waiting for transfers between devices, local(): other = lax.ppermute(table, 'seq', [(s, s ^ step) for s in range(seq_size)])  6.38 us
    ppermute x6, starting transfers between devices, sibling(): return lax.ppermute(array, 'seq', [(s, s ^ 1) for s in range(seq_size)])  4.94 us
  transfers between devices with their start and end apart: 22, of which 7 were waited for; matrix products, arithmetic and copies ran while one was open for 16% of the time, Pallas kernels for 12%

profile of v3, /device:TPU:16, one launch (start us, length us, event | category | flops | bytes accessed | tf_op | source)
XLA Modules:
  0.0 145.8 jit_solution(3841673718439944037)
XLA Ops:
  6.5 1.4 fusion
  7.9 2.1 %fusion.2.rest_0_ = bf16[128,2304]{1,0:T(8,128)(2,1)} fusion(bf16[128,2304]{1,0:T(8,128)(2,1)} %param.10, f32[2304]{0:T(1024)} %param.11, f32[128]{0:T(128)S(1)} %add_rsqrt_fusion.1), kind=kLoop, calls=%fused_computation.5 | loop fusion | flops 1179648 | bytes 1189376 | tf_op jit(solution)/shard_map/convert_element_type | solution.py:251
  10.0 1.5 %collective-permute-start.3 = (bf16[128,2304]{1,0:T(8,128)(2,1)}, bf16[128,2304]{1,0:T(8,128)(2,1)}, u32[]{:S(2)}, u32[]{:S(2)}) collective-permute-start(bf16[128,2304]{1,0:T(8,128)(2,1)} %fusion.2.rest_0_), channel_id=1, source_target_pairs={{0,1},{1,0},{2,3},{3,2},{4,5},{5,4},{6,7},{7,6},{8,9},{9,8},{10,11... | collective-permute-start | bytes 1769480 | tf_op jit(solution)/shard_map/ppermute | solution.py:241
  11.5 1.5 %collective-permute-start.4 = (bf16[128,2304]{1,0:T(8,128)(2,1)}, bf16[128,2304]{1,0:T(8,128)(2,1)}, u32[]{:S(2)}, u32[]{:S(2)}) collective-permute-start(bf16[128,2304]{1,0:T(8,128)(2,1)} %fusion.2.rest_0_), channel_id=1, source_target_pairs={{0,2},{1,3},{2,0},{3,1},{4,6},{5,7},{6,4},{7,5},{8,10},{9,11},{10,... | collective-permute-start | bytes 1769480 | tf_op jit(solution)/shard_map/ppermute | solution.py:241
  13.1 0.7 constant_dynamic-slice_fusion
  13.9 1.8 %constant_dynamic-slice_fusion.1.w_ref = bf16[2304,512]{1,0:T(8,128)(2,1)S(1)} fusion(bf16[2304,2048]{1,0:T(8,128)(2,1)} %param.14, s32[]{:T(128)S(6)} %select_n.201), kind=kLoop, calls=%fused_computation.79 | loop fusion | bytes 4718596 | tf_op jit(solution)/shard_map/dynamic_slice | solution.py:304
  15.8 1.6 %collective-permute-start.1 = (s32[2,528]{1,0:T(2,128)S(1)}, s32[2,528]{1,0:T(2,128)S(1)}, u32[]{:S(2)}, u32[]{:S(2)}) collective-permute-start(s32[2,528]{1,0:T(2,128)S(1)} %pad_add_fusion.7), channel_id=1, source_target_pairs={{0,8},{4,12},{8,0},{12,4},{16,24},{20,28},{24,16},{28,20},{1,9},{5... | collective-permute-start | bytes 12680 | tf_op jit(solution)/shard_map/ppermute | solution.py:269
  17.4 2.0 %collective-permute-done.1 = s32[2,528]{1,0:T(2,128)S(1)} collective-permute-done((s32[2,528]{1,0:T(2,128)S(1)}, s32[2,528]{1,0:T(2,128)S(1)}, u32[]{:S(2)}, u32[]{:S(2)}) %collective-permute-start.1) | collective-permute-done | bytes 4256 | tf_op jit(solution)/shard_map/ppermute | solution.py:269
  20.0 4.3 %collective-permute-done.2 = s32[4,528]{1,0:T(4,128)S(1)} collective-permute-done((s32[4,528]{1,0:T(4,128)S(1)}, s32[4,528]{1,0:T(4,128)S(1)}, u32[]{:S(2)}, u32[]{:S(2)}) %collective-permute-start.2) | collective-permute-done | bytes 8480 | tf_op jit(solution)/shard_map/ppermute | solution.py:269
  27.3 0.8 convert_reduce_fusion.2
  28.8 0.9 fusion.16
  29.7 1.7 %multiply_sine_fusion = (f32[512,128]{1,0:T(8,128)S(1)}, f32[512,128]{1,0:T(8,128)}) fusion(f32[128]{0:T(128)S(1)} %negate_power_fusion, f32[512]{0:T(512)S(1)} %get-tuple-element.50), kind=kLoop, calls=%fused_computation.26 | loop fusion | flops 65536 | bytes 526848 | tf_op jit(solution)/shard_map/sin | solution.py:290
  32.8 1.7 %slice.88 = bf16[64,2304]{1,0:T(8,128)(2,1)} slice(bf16[128,2304]{1,0:T(8,128)(2,1)} %collective-permute-done.3.rest_1_), slice={[0:64], [0:2304]} | slice | bytes 589824 | tf_op jit(solution)/shard_map/slice | solution.py:256
  34.9 1.7 %slice.89 = bf16[64,2304]{1,0:T(8,128)(2,1)} slice(bf16[128,2304]{1,0:T(8,128)(2,1)} %collective-permute-done.4.rest_2_.rest_0_), slice={[64:128], [0:2304]} | slice | bytes 589824 | tf_op jit(solution)/shard_map/slice | solution.py:257
  37.8 1.3 reshape.264.kslot_ref
  39.1 1.3 copy.22
  40.4 1.2 reshape.262.touch_ref
  41.6 1.5 %copy.28.qslot_ref = s32[512,1]{1,0:T(8,128)} copy(s32[512,1]{0,1:T(1,128)} %bitcast.37) | data formatting | bytes 4096 | tf_op jit(solution)/shard_map/broadcast_in_dim | solution.py:184
  43.1 1.5 %copy.27.qseg_ref = s32[512,1]{1,0:T(8,128)} copy(s32[512,1]{0,1:T(1,128)} %bitcast.36) | data formatting | bytes 4096 | tf_op jit(solution)/shard_map/broadcast_in_dim | solution.py:287
  44.7 1.0 fusion.21
  45.7 0.9 copy-done.9
  46.6 2.7 %project.4.rest_0_ = bf16[256,512]{1,0:T(8,128)(2,1)} custom-call(s32[1]{0:T(128)} %constant.115.clone.1.which_ref, f32[256,128]{1,0:T(8,128)S(1)} %get-tuple-element.38.cos_ref, f32[256,128]{1,0:T(8,128)S(1)} %copy-done.9, bf16[2304,512]{1,0:T(8,128)(2,1)S(1)} %constant_dynamic-slice_fusion.1.w_ref, bf16[128,2304]{1,0:T(8,128)(2,1)} %fusion.2.rest_0_, ...), custom_call_target="tpu_custom_call" | custom-call | flops 603979776 | bytes 3538944 | tf_op jit(solution)/shard_map/project/pallas_call | solution.py:65
  49.3 3.5 %collective-permute-start.7 = (bf16[256,512]{1,0:T(8,128)(2,1)}, bf16[256,512]{1,0:T(8,128)(2,1)}, u32[]{:S(2)}, u32[]{:S(2)}) collective-permute-start(bf16[256,512]{1,0:T(8,128)(2,1)} %project.4.rest_0_), channel_id=1, source_target_pairs={{0,8},{4,12},{8,16},{12,20},{16,24},{20,28},{1,9},{5,13},{9,17},{1... | collective-permute-start | bytes 786440 | tf_op jit(solution)/shard_map/ppermute | solution.py:323
  52.9 2.8 %project.5.rest_1_ = bf16[256,512]{1,0:T(8,128)(2,1)} custom-call(s32[1]{0:T(128)} %constant.115.clone.1.which_ref, f32[256,128]{1,0:T(8,128)S(1)} %get-tuple-element.37.cos_ref, f32[256,128]{1,0:T(8,128)S(1)} %get-tuple-element.35.sin_ref, bf16[2304,512]{1,0:T(8,128)(2,1)S(1)} %constant_dynamic-slice_fusion.1.w_ref, ...), custom_call_target="tpu_custom_call" | custom-call | flops 603979776 | bytes 3538944 | tf_op jit(solution)/shard_map/project/pallas_call | solution.py:65
  55.8 2.0 %collective-permute-start.8 = (bf16[256,512]{1,0:T(8,128)(2,1)}, bf16[256,512]{1,0:T(8,128)(2,1)}, u32[]{:S(2)}, u32[]{:S(2)}) collective-permute-start(bf16[256,512]{1,0:T(8,128)(2,1)} %project.5.rest_1_), channel_id=1, source_target_pairs={{0,8},{4,12},{8,16},{12,20},{16,24},{20,28},{1,9},{5,13},{9,17},{1... | collective-permute-start | bytes 786440 | tf_op jit(solution)/shard_map/ppermute | solution.py:323
  58.4 3.0 %project.3.q_ref = bf16[2,512,256]{2,1,0:T(8,128)(2,1)S(1)} custom-call(s32[1]{0:T(128)} %constant.115.clone.1.which_ref, f32[512,128]{1,0:T(8,128)S(1)} %copy-done.3, f32[512,128]{1,0:T(8,128)S(1)} %copy-done.2, bf16[2304,512]{1,0:T(8,128)(2,1)S(1)} %copy-done.4, bf16[128,2304]{1,0:T(8,128)(2,1)} %fusion.2.rest_0_, ...), custom_call_target="tpu_custom_call" | custom-call | flops 1207959552 | bytes 4718592 | tf_op jit(solution)/shard_map/project/pallas_call | solution.py:65
  61.4 0.8 copy-done.5
  62.2 1.0 copy-done.6
  63.2 0.9 copy-done.10
  64.2 0.9 copy-done.13
  65.1 1.6 %copy-done.16 = bf16[1,2048,512]{2,1,0:T(8,128)(2,1)S(1)} copy-done((bf16[1,2048,512]{2,1,0:T(8,128)(2,1)S(1)}, bf16[1,2048,512]{2,1,0:T(8,128)(2,1)}, u32[]{:S(2)}) %copy-start.16) | copy-done | bytes 2097176
  66.8 5.7 %attend.3 = (f32[2,512,256]{2,1,0:T(8,128)S(1)}, f32[2,512,128]{2,1,0:T(8,128)S(1)}) custom-call(s32[20]{0:T(128)S(1)} %copy-done.21, bf16[2,512,256]{2,1,0:T(8,128)(2,1)S(1)} %copy-done.6, s32[512,1]{1,0:T(8,128)S(1)} %copy-done.13, s32[512,1]{1,0:T(8,128)S(1)} %copy-done.10, s32[10,1,256]{2,1,0:T(1,128)S(1)} %reshape.263.kseg_ref, ...), custom_call_target="tpu_custom_call" | custom-call | flops 2684354560 | bytes 2621440 | tf_op jit(solution)/shard_map/attend/pallas_call | solution.py:204
  72.5 1.0 copy-done.24
  73.5 0.8 copy-done.28
  74.3 5.4 %collective-permute-start.11 = (bf16[256,512]{1,0:T(8,128)(2,1)}, bf16[256,512]{1,0:T(8,128)(2,1)}, u32[]{:S(2)}, u32[]{:S(2)}) collective-permute-start(bf16[256,512]{1,0:T(8,128)(2,1)} %collective-permute-done.7.rest_2_), channel_id=1, source_target_pairs={{0,8},{4,12},{8,16},{12,20},{16,24},{20,28},{1,9},{5,13},{9,17},{1... | collective-permute-start | bytes 786440 | tf_op jit(solution)/shard_map/ppermute | solution.py:323
  79.7 2.1 %collective-permute-start.12 = (bf16[256,512]{1,0:T(8,128)(2,1)}, bf16[256,512]{1,0:T(8,128)(2,1)}, u32[]{:S(2)}, u32[]{:S(2)}) collective-permute-start(bf16[256,512]{1,0:T(8,128)(2,1)} %collective-permute-done.8.rest_3_), channel_id=1, source_target_pairs={{0,8},{4,12},{8,16},{12,20},{16,24},{20,28},{1,9},{5,13},{9,17},{1... | collective-permute-start | bytes 786440 | tf_op jit(solution)/shard_map/ppermute | solution.py:323
  82.1 3.7 %collective-permute-start.10 = (bf16[256,512]{1,0:T(8,128)(2,1)}, bf16[256,512]{1,0:T(8,128)(2,1)}, u32[]{:S(2)}, u32[]{:S(2)}) collective-permute-start(bf16[256,512]{1,0:T(8,128)(2,1)} %collective-permute-done.8.rest_3_), channel_id=1, source_target_pairs={{0,4},{4,0},{8,12},{12,8},{16,20},{20,16},{24,28},{28,24},{1,5},{5... | collective-permute-start | bytes 786440 | tf_op jit(solution)/shard_map/ppermute | solution.py:326
  85.9 1.0 copy-done.7
  86.9 0.9 copy-done.11
  87.9 0.9 copy-done.14
  88.8 1.2 copy-done.25
  90.1 1.0 copy-done.29
  91.1 3.8 %attend.4 = (f32[2,512,256]{2,1,0:T(8,128)S(1)}, f32[2,512,128]{2,1,0:T(8,128)S(1)}) custom-call(s32[8]{0:T(128)S(1)} %reshape.265.touch_ref, bf16[2,512,256]{2,1,0:T(8,128)(2,1)S(1)} %copy-done.7, s32[512,1]{1,0:T(8,128)S(1)} %copy-done.14, s32[512,1]{1,0:T(8,128)S(1)} %copy-done.11, s32[4,1,256]{2,1,0:T(1,128)S(1)} %pad_add_fusion.11.kseg_ref, ...), custom_call_target="tpu_custom_call" | custom-call | flops 1073741824 | bytes 1048576 | tf_op jit(solution)/shard_map/attend/pallas_call | solution.py:204
  94.9 1.0 copy-done.22
  95.9 0.8 copy-done.26
  97.7 0.7 collective-permute-done.15.rest_4_
  99.9 1.0 copy-done.8
  100.9 0.9 copy-done.12
  101.9 0.9 copy-done.18
  102.8 0.9 copy-done.20
  103.8 1.2 copy-done.23
  105.0 1.0 copy-done.27
  106.0 8.0 %attend.5 = bf16[512,512]{1,0:T(8,128)(2,1)S(1)} custom-call(s32[12]{0:T(128)S(1)} %reshape.261.touch_ref, bf16[2,512,256]{2,1,0:T(8,128)(2,1)S(1)} %copy-done.8, s32[512,1]{1,0:T(8,128)S(1)} %copy-done.14, s32[512,1]{1,0:T(8,128)S(1)} %copy-done.12, s32[6,1,256]{2,1,0:T(1,128)S(1)} %pad_add_fusion.5.kseg_ref, s32[6,1,256]{2,1,0:T(1,128)S(1)} %pad_add_fusion.6.kslot_ref, ...), custom_call_target="tpu_custom_call" | custom-call | flops 1610612736 | bytes 1572864 | tf_op jit(solution)/shard_map/attend/pallas_call | solution.py:204
  114.0 0.8 fusion.23
  115.0 2.1 %collective-permute-start.17 = (bf16[256,1152]{1,0:T(8,128)(2,1)S(1)}, bf16[256,1152]{1,0:T(8,128)(2,1)S(1)}, u32[]{:S(2)}, u32[]{:S(2)}) collective-permute-start(bf16[256,1152]{1,0:T(8,128)(2,1)S(1)} %pad_maximum_fusion.1), channel_id=1, source_target_pairs={{0,1},{1,0},{2,3},{3,2},{4,5},{5,4},{6,7},{7,6},{8,9},{9,8},{10,11... | collective-permute-start | bytes 1769480 | tf_op jit(solution)/shard_map/ppermute | solution.py:241
  117.0 0.8 fusion.4
  118.0 1.9 %collective-permute-start.19 = (bf16[256,1152]{1,0:T(8,128)(2,1)S(1)}, bf16[256,1152]{1,0:T(8,128)(2,1)S(1)}, u32[]{:S(2)}, u32[]{:S(2)}) collective-permute-start(bf16[256,1152]{1,0:T(8,128)(2,1)S(1)} %slice.128), channel_id=1, source_target_pairs={{0,2},{1,3},{2,0},{3,1},{4,6},{5,7},{6,4},{7,5},{8,10},{9,11},{10,... | collective-permute-start | bytes 1769480 | tf_op jit(solution)/shard_map/ppermute | solution.py:241
  119.9 6.8 %collective-permute-done.17 = bf16[256,1152]{1,0:T(8,128)(2,1)S(1)} collective-permute-done((bf16[256,1152]{1,0:T(8,128)(2,1)S(1)}, bf16[256,1152]{1,0:T(8,128)(2,1)S(1)}, u32[]{:S(2)}, u32[]{:S(2)}) %collective-permute-start.17) | collective-permute-done | bytes 589856 | tf_op jit(solution)/shard_map/ppermute | solution.py:241
  126.9 2.4 %collective-permute-start.18 = (bf16[128,1152]{1,0:T(8,128)(2,1)S(1)}, bf16[128,1152]{1,0:T(8,128)(2,1)S(1)}, u32[]{:S(2)}, u32[]{:S(2)}) collective-permute-start(bf16[128,1152]{1,0:T(8,128)(2,1)S(1)} %fusion.11), channel_id=1, source_target_pairs={{0,2},{1,3},{2,0},{3,1},{4,6},{5,7},{6,4},{7,5},{8,10},{9,11},{10,... | collective-permute-start | bytes 884744 | tf_op jit(solution)/shard_map/ppermute | solution.py:241
  129.3 1.4 collective-permute-done.19
  130.8 1.2 collective-permute-start.20
  132.0 2.0 %collective-permute-done.18 = bf16[128,1152]{1,0:T(8,128)(2,1)S(1)} collective-permute-done((bf16[128,1152]{1,0:T(8,128)(2,1)S(1)}, bf16[128,1152]{1,0:T(8,128)(2,1)S(1)}, u32[]{:S(2)}, u32[]{:S(2)}) %collective-permute-start.18) | collective-permute-done | bytes 294944 | tf_op jit(solution)/shard_map/ppermute | solution.py:241
  134.1 3.5 %collective-permute-done.20 = bf16[128,1152]{1,0:T(8,128)(2,1)S(1)} collective-permute-done((bf16[128,1152]{1,0:T(8,128)(2,1)S(1)}, bf16[128,1152]{1,0:T(8,128)(2,1)S(1)}, u32[]{:S(2)}, u32[]{:S(2)}) %collective-permute-start.20) | collective-permute-done | bytes 294944 | tf_op jit(solution)/shard_map/ppermute | solution.py:241
  137.9 1.1 fusion.3
  (209 shorter events, 11.1 us)
Async XLA Ops:
  6.5 6.6 %copy-start = (bf16[4,256,512]{2,1,0:T(8,128)(2,1)S(1)}, bf16[4,256,512]{2,1,0:T(8,128)(2,1)}, u32[]{:S(2)}) copy-start(bf16[4,256,512]{2,1,0:T(8,128)(2,1)} %param.16) | copy-start | bytes 3145732
  6.5 6.5 %copy-start.57 = (s32[512]{0:T(512)S(1)}, s32[512]{0:T(512)}, u32[]{:S(2)}) copy-start(s32[512]{0:T(512)} %param.17) | copy-start | bytes 6148
  6.5 6.5 %copy-start.59 = (s32[16]{0:T(128)S(1)}, s32[16]{0:T(128)}, u32[]{:S(2)}) copy-start(s32[16]{0:T(128)} %param.19) | copy-start | bytes 196
  6.5 55.6 %all-gather.3.cloned.1.call-start = ((), (), s32[]{:S(2)}) async-start(), calls=%async_computation | async-start | bytes 2359296 | tf_op jit(solution)/shard_map/all_gather | solution.py:263
  10.0 22.8 %collective-permute-start.3 = (bf16[128,2304]{1,0:T(8,128)(2,1)}, bf16[128,2304]{1,0:T(8,128)(2,1)}, u32[]{:S(2)}, u32[]{:S(2)}) collective-permute-start(bf16[128,2304]{1,0:T(8,128)(2,1)} %fusion.2.rest_0_), channel_id=1, source_target_pairs={{0,1},{1,0},{2,3},{3,2},{4,5},{5,4},{6,7},{7,6},{8,9},{9,8},{10,11... | collective-permute-start | bytes 1769480 | tf_op jit(solution)/shard_map/ppermute | solution.py:241
  11.5 23.4 %collective-permute-start.4 = (bf16[128,2304]{1,0:T(8,128)(2,1)}, bf16[128,2304]{1,0:T(8,128)(2,1)}, u32[]{:S(2)}, u32[]{:S(2)}) collective-permute-start(bf16[128,2304]{1,0:T(8,128)(2,1)} %fusion.2.rest_0_), channel_id=1, source_target_pairs={{0,2},{1,3},{2,0},{3,1},{4,6},{5,7},{6,4},{7,5},{8,10},{9,11},{10,... | collective-permute-start | bytes 1769480 | tf_op jit(solution)/shard_map/ppermute | solution.py:241
  13.0 2.7 %collective-permute-start = (s32[1,528]{1,0:T(1,128)S(1)}, s32[1,528]{1,0:T(1,128)S(1)}, u32[]{:S(2)}, u32[]{:S(2)}) collective-permute-start(s32[1,528]{1,0:T(1,128)S(1)} %broadcast_in_dim.37), channel_id=1, source_target_pairs={{0,4},{4,0},{8,12},{12,8},{16,20},{20,16},{24,28},{28,24},{1,5},{5... | collective-permute-start | bytes 6344 | tf_op jit(solution)/shard_map/ppermute | solution.py:269
  13.9 11.3 %copy-start.60 = (s32[64]{0:T(128)S(1)}, s32[64]{0:T(128)}, u32[]{:S(2)}) copy-start(s32[64]{0:T(128)} %param.18) | copy-start | bytes 772
  15.8 3.7 %collective-permute-start.1 = (s32[2,528]{1,0:T(2,128)S(1)}, s32[2,528]{1,0:T(2,128)S(1)}, u32[]{:S(2)}, u32[]{:S(2)}) collective-permute-start(s32[2,528]{1,0:T(2,128)S(1)} %pad_add_fusion.7), channel_id=1, source_target_pairs={{0,8},{4,12},{8,0},{12,4},{16,24},{20,28},{24,16},{28,20},{1,9},{5... | collective-permute-start | bytes 12680 | tf_op jit(solution)/shard_map/ppermute | solution.py:269
  19.5 4.9 %collective-permute-start.2 = (s32[4,528]{1,0:T(4,128)S(1)}, s32[4,528]{1,0:T(4,128)S(1)}, u32[]{:S(2)}, u32[]{:S(2)}) collective-permute-start(s32[4,528]{1,0:T(4,128)S(1)} %pad_add_fusion.2), channel_id=1, source_target_pairs={{0,16},{4,20},{8,24},{12,28},{16,0},{20,4},{24,8},{28,12},{1,17},{... | collective-permute-start | bytes 25352 | tf_op jit(solution)/shard_map/ppermute | solution.py:269
  25.8 2.3 %copy-start.34 = (s32[512]{0:T(512)}, s32[512]{0:T(512)S(1)}, u32[]{:S(2)}) copy-start(s32[512]{0:T(512)S(1)} %dynamic_slice.52) | copy-start | bytes 6148
  26.6 1.5 %copy-start.42 = (s32[512]{0:T(512)}, s32[512]{0:T(512)S(1)}, u32[]{:S(2)}) copy-start(s32[512]{0:T(512)S(1)} %get-tuple-element.48) | copy-start | bytes 6148
  26.6 2.1 %copy-start.36 = (s32[512]{0:T(512)}, s32[512]{0:T(512)S(1)}, u32[]{:S(2)}) copy-start(s32[512]{0:T(512)S(1)} %get-tuple-element.51) | copy-start | bytes 6148
  26.6 2.1 %copy-start.40 = (s32[512]{0:T(512)}, s32[512]{0:T(512)S(1)}, u32[]{:S(2)}) copy-start(s32[512]{0:T(512)S(1)} %get-tuple-element.47) | copy-start | bytes 6148
  26.7 1.4 copy-start.44
  27.0 4.5 %copy-start.51 = (s32[2]{0:T(128)}, s32[2]{0:T(128)S(1)}, u32[]{:S(2)}) copy-start(s32[2]{0:T(128)S(1)} %reduce_max.44) | copy-start | bytes 28
  27.3 4.1 %copy-start.53 = (s32[2]{0:T(128)}, s32[2]{0:T(128)S(1)}, u32[]{:S(2)}) copy-start(s32[2]{0:T(128)S(1)} %get-tuple-element.29) | copy-start | bytes 28
  27.3 4.1 %copy-start.55 = (s32[2]{0:T(128)}, s32[2]{0:T(128)S(1)}, u32[]{:S(2)}) copy-start(s32[2]{0:T(128)S(1)} %get-tuple-element.30) | copy-start | bytes 28
  27.3 4.1 %copy-start.32 = (s32[2560]{0:T(1024)}, s32[2560]{0:T(1024)S(1)}, u32[]{:S(2)}) copy-start(s32[2560]{0:T(1024)S(1)} %pad_add_fusion.1) | copy-start | bytes 30724
  28.7 2.7 %copy-start.33 = (s32[2560]{0:T(1024)}, s32[2560]{0:T(1024)S(1)}, u32[]{:S(2)}) copy-start(s32[2560]{0:T(1024)S(1)} %concatenate.116) | copy-start | bytes 30724
  34.5 18.4 %collective-permute-start.5 = (bf16[64,2304]{1,0:T(8,128)(2,1)}, bf16[64,2304]{1,0:T(8,128)(2,1)}, u32[]{:S(2)}, u32[]{:S(2)}) collective-permute-start(bf16[64,2304]{1,0:T(8,128)(2,1)} %slice.88), channel_id=1, source_target_pairs={{0,2},{1,3},{2,0},{3,1},{4,6},{5,7},{6,4},{7,5},{8,10},{9,11},{10,... | collective-permute-start | bytes 884744 | tf_op jit(solution)/shard_map/ppermute | solution.py:241
  36.6 16.3 %collective-permute-start.6 = (bf16[64,2304]{1,0:T(8,128)(2,1)}, bf16[64,2304]{1,0:T(8,128)(2,1)}, u32[]{:S(2)}, u32[]{:S(2)}) collective-permute-start(bf16[64,2304]{1,0:T(8,128)(2,1)} %slice.89), channel_id=1, source_target_pairs={{0,1},{1,0},{2,3},{3,2},{4,5},{5,4},{6,7},{7,6},{8,9},{9,8},{10,11... | collective-permute-start | bytes 884744 | tf_op jit(solution)/shard_map/ppermute | solution.py:241
  49.3 25.0 %collective-permute-start.7 = (bf16[256,512]{1,0:T(8,128)(2,1)}, bf16[256,512]{1,0:T(8,128)(2,1)}, u32[]{:S(2)}, u32[]{:S(2)}) collective-permute-start(bf16[256,512]{1,0:T(8,128)(2,1)} %project.4.rest_0_), channel_id=1, source_target_pairs={{0,8},{4,12},{8,16},{12,20},{16,24},{20,28},{1,9},{5,13},{9,17},{1... | collective-permute-start | bytes 786440 | tf_op jit(solution)/shard_map/ppermute | solution.py:323
  52.8 33.0 %collective-permute-start.13 = (bf16[256,512]{1,0:T(8,128)(2,1)}, bf16[256,512]{1,0:T(8,128)(2,1)}, u32[]{:S(2)}, u32[]{:S(2)}) collective-permute-start(bf16[256,512]{1,0:T(8,128)(2,1)} %project.4.rest_0_), channel_id=1, source_target_pairs={{0,4},{4,0},{8,12},{12,8},{16,20},{20,16},{24,28},{28,24},{1,5},{5... | collective-permute-start | bytes 786440 | tf_op jit(solution)/shard_map/ppermute | solution.py:326
  52.9 5.5 %copy-start.2 = (f32[512,128]{1,0:T(8,128)S(1)}, f32[512,128]{1,0:T(8,128)}, u32[]{:S(2)}) copy-start(f32[512,128]{1,0:T(8,128)} %copy-done.1) | copy-start | bytes 786436
  52.9 5.5 %copy-start.3 = (f32[512,128]{1,0:T(8,128)S(1)}, f32[512,128]{1,0:T(8,128)}, u32[]{:S(2)}) copy-start(f32[512,128]{1,0:T(8,128)} %get-tuple-element.56.cos_ref) | copy-start | bytes 786436
  52.9 5.5 %copy-start.4 = (bf16[2304,512]{1,0:T(8,128)(2,1)S(1)}, bf16[2304,512]{1,0:T(8,128)(2,1)}, u32[]{:S(2)}) copy-start(bf16[2304,512]{1,0:T(8,128)(2,1)} %w_ref.1) | copy-start | bytes 7077892
  55.8 6.4 %copy-start.15 = (s32[10,1,256]{2,1,0:T(1,128)S(1)}, s32[10,1,256]{2,1,0:T(1,128)}, u32[]{:S(2)}) copy-start(s32[10,1,256]{2,1,0:T(1,128)} %reshape.264.kslot_ref) | copy-start | bytes 30724
  55.8 6.4 %copy-start.21 = (s32[20]{0:T(128)S(1)}, s32[20]{0:T(128)}, u32[]{:S(2)}) copy-start(s32[20]{0:T(128)} %reshape.262.touch_ref) | copy-start | bytes 244
  55.8 18.5 %collective-permute-start.8 = (bf16[256,512]{1,0:T(8,128)(2,1)}, bf16[256,512]{1,0:T(8,128)(2,1)}, u32[]{:S(2)}, u32[]{:S(2)}) collective-permute-start(bf16[256,512]{1,0:T(8,128)(2,1)} %project.5.rest_1_), channel_id=1, source_target_pairs={{0,8},{4,12},{8,16},{12,20},{16,24},{20,28},{1,9},{5,13},{9,17},{1... | collective-permute-start | bytes 786440 | tf_op jit(solution)/shard_map/ppermute | solution.py:323
  57.8 28.1 %collective-permute-start.14 = (bf16[256,512]{1,0:T(8,128)(2,1)}, bf16[256,512]{1,0:T(8,128)(2,1)}, u32[]{:S(2)}, u32[]{:S(2)}) collective-permute-start(bf16[256,512]{1,0:T(8,128)(2,1)} %project.5.rest_1_), channel_id=1, source_target_pairs={{0,4},{4,0},{8,12},{12,8},{16,20},{20,16},{24,28},{28,24},{1,5},{5... | collective-permute-start | bytes 786440 | tf_op jit(solution)/shard_map/ppermute | solution.py:326
  62.2 1.0 copy-start.6
  65.1 1.6 %copy-start.16 = (bf16[1,2048,512]{2,1,0:T(8,128)(2,1)S(1)}, bf16[1,2048,512]{2,1,0:T(8,128)(2,1)}, u32[]{:S(2)}) copy-start(bf16[1,2048,512]{2,1,0:T(8,128)(2,1)} %all-gather.3.cloned.1.call-done) | copy-start | bytes 6291460
  66.7 15.1 %copy-start.41 = (s32[512]{0:T(512)S(1)}, s32[512]{0:T(512)}, u32[]{:S(2)}) copy-start(s32[512]{0:T(512)} %copy-done.40) | copy-start | bytes 6148
  66.7 15.1 %copy-start.43 = (s32[512]{0:T(512)S(1)}, s32[512]{0:T(512)}, u32[]{:S(2)}) copy-start(s32[512]{0:T(512)} %copy-done.42) | copy-start | bytes 6148
  66.7 15.1 %copy-start.58 = (s32[2,4]{1,0:T(2,128)S(1)}, s32[2,4]{1,0:T(2,128)}, u32[]{:S(2)}) copy-start(s32[2,4]{1,0:T(2,128)} %convert_reduce_fusion.2) | copy-start | bytes 100
  66.7 15.2 %copy-start.39 = (s32[512]{0:T(512)S(1)}, s32[512]{0:T(512)}, u32[]{:S(2)}) copy-start(s32[512]{0:T(512)} %get-tuple-element.54) | copy-start | bytes 6148
  66.7 15.2 %copy-start.38 = (s32[512]{0:T(512)S(1)}, s32[512]{0:T(512)}, u32[]{:S(2)}) copy-start(s32[512]{0:T(512)} %get-tuple-element.53) | copy-start | bytes 6148
  66.7 15.2 %copy-start.37 = (s32[512]{0:T(512)S(1)}, s32[512]{0:T(512)}, u32[]{:S(2)}) copy-start(s32[512]{0:T(512)} %get-tuple-element.52) | copy-start | bytes 6148
  74.3 22.4 %collective-permute-start.11 = (bf16[256,512]{1,0:T(8,128)(2,1)}, bf16[256,512]{1,0:T(8,128)(2,1)}, u32[]{:S(2)}, u32[]{:S(2)}) collective-permute-start(bf16[256,512]{1,0:T(8,128)(2,1)} %collective-permute-done.7.rest_2_), channel_id=1, source_target_pairs={{0,8},{4,12},{8,16},{12,20},{16,24},{20,28},{1,9},{5,13},{9,17},{1... | collective-permute-start | bytes 786440 | tf_op jit(solution)/shard_map/ppermute | solution.py:323
  79.7 17.0 %collective-permute-start.12 = (bf16[256,512]{1,0:T(8,128)(2,1)}, bf16[256,512]{1,0:T(8,128)(2,1)}, u32[]{:S(2)}, u32[]{:S(2)}) collective-permute-start(bf16[256,512]{1,0:T(8,128)(2,1)} %collective-permute-done.8.rest_3_), channel_id=1, source_target_pairs={{0,8},{4,12},{8,16},{12,20},{16,24},{20,28},{1,9},{5,13},{9,17},{1... | collective-permute-start | bytes 786440 | tf_op jit(solution)/shard_map/ppermute | solution.py:323
  82.0 15.3 %copy-start.52 = (s32[2]{0:T(128)S(1)}, s32[2]{0:T(128)}, u32[]{:S(2)}) copy-start(s32[2]{0:T(128)} %copy-done.51) | copy-start | bytes 28
  82.0 15.3 %copy-start.54 = (s32[2]{0:T(128)S(1)}, s32[2]{0:T(128)}, u32[]{:S(2)}) copy-start(s32[2]{0:T(128)} %copy-done.53) | copy-start | bytes 28
  82.0 15.2 %copy-start.56 = (s32[2]{0:T(128)S(1)}, s32[2]{0:T(128)}, u32[]{:S(2)}) copy-start(s32[2]{0:T(128)} %copy-done.55) | copy-start | bytes 28
  82.0 15.2 %copy-start.35 = (s32[6,256]{1,0:T(8,128)S(1)}, s32[6,256]{1,0:T(8,128)}, u32[]{:S(2)}) copy-start(s32[6,256]{1,0:T(8,128)} %pad_add_fusion.3) | copy-start | bytes 18436
  82.0 15.7 %copy-start.45 = (s32[512]{0:T(512)S(1)}, s32[512]{0:T(512)}, u32[]{:S(2)}) copy-start(s32[512]{0:T(512)} %copy-done.44) | copy-start | bytes 6148
  82.0 15.6 %copy-start.47 = (s32[512]{0:T(512)S(1)}, s32[512]{0:T(512)}, u32[]{:S(2)}) copy-start(s32[512]{0:T(512)} %copy-done.46) | copy-start | bytes 6148
  82.0 15.6 %copy-start.49 = (s32[512]{0:T(512)S(1)}, s32[512]{0:T(512)}, u32[]{:S(2)}) copy-start(s32[512]{0:T(512)} %copy-done.48) | copy-start | bytes 6148
  82.1 15.6 %collective-permute-start.10 = (bf16[256,512]{1,0:T(8,128)(2,1)}, bf16[256,512]{1,0:T(8,128)(2,1)}, u32[]{:S(2)}, u32[]{:S(2)}) collective-permute-start(bf16[256,512]{1,0:T(8,128)(2,1)} %collective-permute-done.8.rest_3_), channel_id=1, source_target_pairs={{0,4},{4,0},{8,12},{12,8},{16,20},{20,16},{24,28},{28,24},{1,5},{5... | collective-permute-start | bytes 786440 | tf_op jit(solution)/shard_map/ppermute | solution.py:326
  85.8 11.9 %collective-permute-start.9 = (bf16[256,512]{1,0:T(8,128)(2,1)}, bf16[256,512]{1,0:T(8,128)(2,1)}, u32[]{:S(2)}, u32[]{:S(2)}) collective-permute-start(bf16[256,512]{1,0:T(8,128)(2,1)} %collective-permute-done.7.rest_2_), channel_id=1, source_target_pairs={{0,4},{4,0},{8,12},{12,8},{16,20},{20,16},{24,28},{28,24},{1,5},{5... | collective-permute-start | bytes 786440 | tf_op jit(solution)/shard_map/ppermute | solution.py:326
  85.9 1.0 copy-start.7
  88.8 1.2 copy-start.25
  90.1 1.0 copy-start.29
  96.7 1.7 %collective-permute-start.15 = (bf16[256,512]{1,0:T(8,128)(2,1)}, bf16[256,512]{1,0:T(8,128)(2,1)S(1)}, u32[]{:S(2)}, u32[]{:S(2)}) collective-permute-start(bf16[256,512]{1,0:T(8,128)(2,1)} %collective-permute-done.11.rest_2_), channel_id=1, source_target_pairs={{0,4},{4,0},{8,12},{12,8},{16,20},{20,16},{24,28},{28,24},{1,5},{5... | collective-permute-start | bytes 786440 | tf_op jit(solution)/shard_map/ppermute | solution.py:326
  96.7 2.5 %collective-permute-start.16 = (bf16[256,512]{1,0:T(8,128)(2,1)}, bf16[256,512]{1,0:T(8,128)(2,1)S(1)}, u32[]{:S(2)}, u32[]{:S(2)}) collective-permute-start(bf16[256,512]{1,0:T(8,128)(2,1)} %collective-permute-done.12.rest_3_), channel_id=1, source_target_pairs={{0,4},{4,0},{8,12},{12,8},{16,20},{20,16},{24,28},{28,24},{1,5},{5... | collective-permute-start | bytes 786440 | tf_op jit(solution)/shard_map/ppermute | solution.py:326
  99.9 1.0 copy-start.8
  103.8 1.2 copy-start.23
  106.0 8.0 %copy-start.31 = (bf16[512,2304]{1,0:T(8,128)(2,1)S(1)}, bf16[512,2304]{1,0:T(8,128)(2,1)}, u32[]{:S(2)}) copy-start(bf16[512,2304]{1,0:T(8,128)(2,1)} %param.15) | copy-start | bytes 7077892
  115.0 11.7 %collective-permute-start.17 = (bf16[256,1152]{1,0:T(8,128)(2,1)S(1)}, bf16[256,1152]{1,0:T(8,128)(2,1)S(1)}, u32[]{:S(2)}, u32[]{:S(2)}) collective-permute-start(bf16[256,1152]{1,0:T(8,128)(2,1)S(1)} %pad_maximum_fusion.1), channel_id=1, source_target_pairs={{0,1},{1,0},{2,3},{3,2},{4,5},{5,4},{6,7},{7,6},{8,9},{9,8},{10,11... | collective-permute-start | bytes 1769480 | tf_op jit(solution)/shard_map/ppermute | solution.py:241
  118.0 12.7 %collective-permute-start.19 = (bf16[256,1152]{1,0:T(8,128)(2,1)S(1)}, bf16[256,1152]{1,0:T(8,128)(2,1)S(1)}, u32[]{:S(2)}, u32[]{:S(2)}) collective-permute-start(bf16[256,1152]{1,0:T(8,128)(2,1)S(1)} %slice.128), channel_id=1, source_target_pairs={{0,2},{1,3},{2,0},{3,1},{4,6},{5,7},{6,4},{7,5},{8,10},{9,11},{10,... | collective-permute-start | bytes 1769480 | tf_op jit(solution)/shard_map/ppermute | solution.py:241
  126.9 7.1 %collective-permute-start.18 = (bf16[128,1152]{1,0:T(8,128)(2,1)S(1)}, bf16[128,1152]{1,0:T(8,128)(2,1)S(1)}, u32[]{:S(2)}, u32[]{:S(2)}) collective-permute-start(bf16[128,1152]{1,0:T(8,128)(2,1)S(1)} %fusion.11), channel_id=1, source_target_pairs={{0,2},{1,3},{2,0},{3,1},{4,6},{5,7},{6,4},{7,5},{8,10},{9,11},{10,... | collective-permute-start | bytes 884744 | tf_op jit(solution)/shard_map/ppermute | solution.py:241
  130.8 6.8 %collective-permute-start.20 = (bf16[128,1152]{1,0:T(8,128)(2,1)S(1)}, bf16[128,1152]{1,0:T(8,128)(2,1)S(1)}, u32[]{:S(2)}, u32[]{:S(2)}) collective-permute-start(bf16[128,1152]{1,0:T(8,128)(2,1)S(1)} %fusion.9), channel_id=1, source_target_pairs={{0,1},{1,0},{2,3},{3,2},{4,5},{5,4},{6,7},{7,6},{8,9},{9,8},{10,11... | collective-permute-start | bytes 884744 | tf_op jit(solution)/shard_map/ppermute | solution.py:241
  134.1 3.8 %copy-start.30 = (bf16[128,2304]{1,0:T(8,128)(2,1)S(1)}, bf16[128,2304]{1,0:T(8,128)(2,1)}, u32[]{:S(2)}) copy-start(bf16[128,2304]{1,0:T(8,128)(2,1)} %param.10) | copy-start | bytes 1769476
  134.1 3.8 %copy-start.50 = (f32[2304]{0:T(1024)S(1)}, f32[2304]{0:T(1024)}, u32[]{:S(2)}) copy-start(f32[2304]{0:T(1024)} %param.12) | copy-start | bytes 27652
  (19 other events, 16.3 us)
Sparse Core Ops, SparseCore 0:
  14.0 27.8 all-gather.2
